TPU v7x, 32 devices: a whole 2x2x4 slice. The times are simulated.
32 devices in a mesh: span: 2 (over x), dom: 16 (over z, y, core).
Axes of the slice: x: 2, y: 2, z: 4, core: 2. Of those that a mesh axis runs over, the one named last changes fastest.
Arguments:
- krylov: float32 [20, 5, 8, 4096], P(None, None, 'span', 'dom'), may hold values from -75 to 75
- limiter: float32 [5, 8, 4096], P(None, 'span', 'dom'), may hold values from 0 to 1
- pseudo_diag: float32 [8, 4096], P('span', 'dom'), may hold values from 1 to 4
- face_states: float32 [2, 5, 8, 8192], P(None, None, 'span', 'dom'), may hold values from -2 to 13.5, as said below
- face_angle: float32 [8192], P('dom'), may hold values from -3.140625 to 3.140625
- face_area: float32 [8192], P('dom'), may hold values from 0.3 to 1.5
- slope_weight: float32 [8192], P('dom'), may hold values from 0.05 to 0.3
- span_coupling: float32 [4096], P('dom'), may hold values from 0.2 to 1
- face_cells: int32 [2, 8192], P(None, 'dom'), may hold values from 0 to 767, as said below
- send_list: int32 [4, 2048], P(None, 'dom'), may hold values from 0 to 255, as said below
- send_count: int32 [4, 16], P(None, 'dom'), may hold values from 0 to 128, as said below
Outputs:
- new_vectors: float32 [3, 5, 8, 4096], P(None, None, 'span', 'dom')
- hessenberg: float32 [3, 23], replicated
Inputs may be any that keep to these rules, and one draw needn't show every extreme that they name: `face_cells`: row 0 names owned cells, below 256. A row 1 entry at or above 256 is a ghost slot 256 + j * 128 + k that is live: its sender block exists and k is below that sender's send_count; every live slot of a block is named by exactly one face; a row 1 entry below 256 differs from row 0. `send_list`: entries of one peer slot's list of one block are distinct owned cells. `send_count`: A slot whose receiving block (dom index plus its offset) does not exist has count 0; some block sends a full 128 in slots 2 and 3. `face_states`: each saved state has density and pressure 0.5 or more.
All inputs are finite; a program needn't handle non-finite values.
Results may differ from a plain program's by a relative error of at most 0.00085.
Values sent between devices are 32-bit elements; how exact they have to be, the bound alone decides.
No kernel may reach another device: no remote copies, remote signals or barrier semaphores. Data moves between devices by JAX's collectives and lax.ppermute only.
A program may use at most 64 MiB of HBM per device.

v0:
```python
import functools

import jax
import jax.numpy as jnp
from jax import lax
from jax.experimental import pallas as pl
from jax.experimental.pallas import tpu as pltpu
from jax.sharding import PartitionSpec as P

PRODUCTS = 3
PEERS = 4
EPSILON = 1e-06
GAMMA = 1.4
LANES = 128
DOT_LANES = 28

PIECE_OF_SENDER = (4, 1, 3, 2)
PIECE_OF_HOLDER = (2, 3, 1, 4)

VMEM_LIMIT = 16 * 1024 * 1024
NT = (((1,), (1,)), ((), ()))


def call(kernel, out_shape, *args, smem=(), scratch=()):
    specs = [
        pl.BlockSpec(memory_space=pltpu.SMEM if i in smem else pltpu.VMEM)
        for i in range(len(args))
    ]
    out_specs = jax.tree.map(lambda _: pl.BlockSpec(memory_space=pltpu.VMEM), out_shape)
    return pl.pallas_call(
        kernel,
        out_shape=out_shape,
        in_specs=specs,
        out_specs=out_specs,
        scratch_shapes=list(scratch),
        compiler_params=pltpu.CompilerParams(vmem_limit_bytes=VMEM_LIMIT),
    )(*args)


def f32(*shape):
    return jax.ShapeDtypeStruct(shape, jnp.float32)


def i32(*shape):
    return jax.ShapeDtypeStruct(shape, jnp.int32)


def split_rows(value):
    high = value.astype(jnp.bfloat16).astype(jnp.float32)
    return jnp.concatenate([high, value - high], axis=0).astype(jnp.bfloat16)


def primitives(states_ref, side, nx, ny):
    rho = states_ref[side, 0]
    inverse = 1.0 / rho
    ux = states_ref[side, 1] * inverse
    uy = states_ref[side, 2] * inverse
    uz = states_ref[side, 3] * inverse
    energy = states_ref[side, 4]
    pressure = (GAMMA - 1.0) * (energy - 0.5 * rho * (ux * ux + uy * uy + uz * uz))
    enthalpy = (energy + pressure) * inverse
    speed = jnp.abs(ux * nx + uy * ny) + jnp.sqrt(GAMMA * pressure * inverse)
    return [ux, uy, uz, enthalpy], speed


def prepare_kernel(cells, cap, bits, odd_ref, states_ref, nx_ref, ny_ref, area_ref, slope_ref,
                   face_cells_ref, list_ref, coef_ref, row_ref, index_ref, message_ref):
    faces = nx_ref.shape[1]
    layers = states_ref.shape[2]
    nx, ny = nx_ref[...], ny_ref[...]
    half = 0.5 * area_ref[...]
    left, speed_left = primitives(states_ref, 0, nx, ny)
    right, speed_right = primitives(states_ref, 1, nx, ny)
    bound = half * jnp.maximum(speed_left, speed_right)
    for k, value in enumerate(left + right + [bound]):
        coef_ref[k] = value
    rows = [half * nx, half * ny, slope_ref[...]]
    for k, value in enumerate(rows):
        row_ref[k : k + 1, :] = value

    is_odd = odd_ref[0] == 1
    owner = face_cells_ref[0:1, :]
    other = face_cells_ref[1:2, :]
    lists = [
        jnp.where(is_odd, list_ref[PEERS - 1 - g : PEERS - g, :], list_ref[g : g + 1, :])
        for g in range(PEERS)
    ]
    ghost = other - cells
    group = jnp.zeros_like(ghost)
    for g in range(1, PEERS):
        group = group + (ghost >= g * cap).astype(jnp.int32)
    mirrored = ghost + (PEERS - 1 - 2 * group) * cap
    slot = jnp.where(jnp.logical_and(is_odd, ghost >= 0), mirrored, ghost)
    index_ref[0:1, :] = owner
    index_ref[1:2, :] = slot + cells
    for g in range(PEERS):
        index_ref[2:3, g * cap : (g + 1) * cap] = lists[g]

    packed = jnp.concatenate(right + [bound] + rows + [owner.astype(jnp.float32)], axis=0)
    count = packed.shape[0]
    named = lax.broadcasted_iota(jnp.int32, (PEERS * cap, faces), 0) == slot
    picked = lax.dot_general(
        split_rows(packed), named.astype(jnp.float32).astype(jnp.bfloat16), NT,
        preferred_element_type=jnp.float32,
    )
    picked = picked[:count] + picked[count:]
    for g in range(PEERS):
        part = picked[:, g * cap : (g + 1) * cap]
        code = part[count - 1 :] * float(1 << bits) + lists[PEERS - 1 - g].astype(jnp.float32)
        message_ref[g * count : (g + 1) * count - 1, :] = part[: count - 1]
        message_ref[(g + 1) * count - 1 : (g + 1) * count, :] = code


def build_kernel(cells, cap, bits, layers, coef_ref, row_ref, index_ref, m0, m1, m2, m3,
                 flux_ref, where_ref, hot_ref):
    messages = (m0, m1, m2, m3)
    faces = coef_ref.shape[2]
    last = m0.shape[0] - 1
    zeros = jnp.zeros((layers, faces), jnp.float32)

    def across(row):
        return jnp.concatenate([m[row : row + 1, :] for m in messages], axis=1)

    def block(k):
        return jnp.concatenate([m[k * layers : (k + 1) * layers, :] for m in messages], axis=1)

    def twice(own, cut):
        return jnp.concatenate(
            [jnp.broadcast_to(own, (layers, faces)), jnp.broadcast_to(cut, (layers, faces))], axis=0
        )

    left = [jnp.concatenate([coef_ref[k], zeros], axis=0) for k in range(4)]
    right = [jnp.concatenate([coef_ref[4 + k], block(k)], axis=0) for k in range(4)]
    bound = jnp.concatenate([coef_ref[8], block(4)], axis=0)
    nx, ny, slope = [twice(row_ref[k : k + 1, :], across(5 * layers + k)) for k in range(3)]
    values = []
    for ux, uy, uz, enthalpy in (left, right):
        values += [ux, uy, uz, enthalpy, ux * nx + uy * ny, 0.5 * (ux * ux + uy * uy + uz * uz)]
    for k, value in enumerate(values + [bound, nx, ny, slope]):
        flux_ref[k] = value

    code = [m[last : last + 1, :].astype(jnp.int32) for m in messages]
    held = jnp.concatenate([lax.shift_right_logical(c, bits) for c in code], axis=1)
    sent = [jnp.bitwise_and(code[PEERS - 1 - g], (1 << bits) - 1) for g in range(PEERS)]
    owner, other, mine = index_ref[0:1, :], index_ref[1:2, :], index_ref[2:3, :]
    ghost = other - cells
    table = [
        jnp.broadcast_to(sent[g] + PIECE_OF_SENDER[g] * cells, (2 * layers, cap)) for g in range(PEERS)
    ]
    found = []
    for f in range(faces // LANES):
        slot = jnp.broadcast_to(ghost[:, f * LANES : (f + 1) * LANES], (2 * layers, LANES))
        low = jnp.bitwise_and(slot, LANES - 1)
        value = jnp.broadcast_to(other[:, f * LANES : (f + 1) * LANES], (2 * layers, LANES))
        for g in range(PEERS):
            picked = jnp.take_along_axis(table[g], low, axis=1, mode="promise_in_bounds")
            inside = jnp.logical_and(slot >= g * cap, slot < (g + 1) * cap)
            value = jnp.where(inside, picked, value)
        found.append(value[0:1])
    far = jnp.concatenate(found, axis=1)
    where_ref[0] = twice(owner, held)
    where_ref[1] = twice(far, mine)
    cell = lax.broadcasted_iota(jnp.int32, (cells, faces), 0)
    used = slope[layers : layers + 1, :] != 0.0
    one = jnp.float32(1.0)
    hot_ref[0] = jnp.where(cell == owner, one, 0.0).astype(jnp.bfloat16)
    hot_ref[1] = jnp.where(cell == other, one, 0.0).astype(jnp.bfloat16)
    hot_ref[2] = jnp.where(cell == jnp.where(used, mine, -1), one, 0.0).astype(jnp.bfloat16)


def gather_jump(pieces, where_ref, layers, tiles, variables, f):
    rows = 2 * layers
    upper = lax.broadcasted_iota(jnp.int32, (rows, LANES), 0) < layers
    near = where_ref[0, :, f * LANES : (f + 1) * LANES]
    far = where_ref[1, :, f * LANES : (f + 1) * LANES]
    near_low, near_tile = jnp.bitwise_and(near, LANES - 1), lax.shift_right_logical(near, 7)
    far_low, far_tile = jnp.bitwise_and(far, LANES - 1), lax.shift_right_logical(far, 7)
    holder = PIECE_OF_HOLDER[f]

    def take(source, index):
        return jnp.take_along_axis(source, index, axis=1, mode="promise_in_bounds")

    jumps = []
    for v in range(variables):
        value = None
        for t in range(tiles):
            source = jnp.where(upper, pieces[0][v][t], pieces[holder][v][t])
            got = take(source, near_low)
            value = got if value is None else jnp.where(near_tile == t, got, value)
        other = None
        for p in range(len(pieces)):
            for t in range(tiles):
                got = take(pieces[p][v][t], far_low)
                other = got if other is None else jnp.where(far_tile == p * tiles + t, got, other)
        jumps.append(value - other)
    return jumps


def doubled(refs, layers, tiles, variables):
    rows = layers * tiles
    pieces = []
    for ref, base in refs:
        piece = []
        for v in range(variables):
            parts = []
            for t in range(tiles):
                start = base + v * rows + t * layers
                part = ref[start : start + layers, :]
                parts.append(jnp.concatenate([part, part], axis=0))
            piece.append(parts)
        pieces.append(piece)
    return pieces


def side_flux(coefs, nx, ny, e):
    ux, uy, uz, enthalpy, normal, kinetic = coefs
    alpha = ux * e[1] + uy * e[2] + uz * e[3] + enthalpy * e[4]
    beta = (GAMMA - 1.0) * (nx * e[1] + ny * e[2] + normal * e[4])
    total = e[0] + alpha
    return [
        beta * kinetic - alpha * normal,
        nx * total + normal * e[1] - beta * ux,
        ny * total + normal * e[2] - beta * uy,
        normal * e[3] - beta * uz,
        beta + normal * e[4],
    ]


def scatter(value, hot_ref, k):
    got = lax.dot_general(split_rows(value), hot_ref[k], NT, preferred_element_type=jnp.float32)
    half = got.shape[0] // 2
    return got[:half] + got[half:]


def to_tiles(value, tiles):
    return jnp.concatenate([value[:, t * LANES : (t + 1) * LANES] for t in range(tiles)], axis=0)


def state_kernel(layers, tiles, variables, bases, x_ref, a_ref, b_ref, c_ref, flux_ref, where_ref,
                 hot_ref, limiter_ref, p_ref, s_ref, left_ref, right_ref):
    rows = layers * tiles
    size = variables * rows
    refs = ((x_ref, bases[0]), (a_ref, bases[1]), (b_ref, bases[2]), (b_ref, bases[2] + size), (c_ref, bases[3]))
    pieces = doubled(refs, layers, tiles, variables)
    faces = flux_ref.shape[2]
    for f in range(faces // LANES):
        lanes = slice(f * LANES, (f + 1) * LANES)
        e = gather_jump(pieces, where_ref, layers, tiles, variables, f)
        coefs = [flux_ref[k, :, lanes] for k in range(15)]
        bound, nx, ny = coefs[12:]
        left = side_flux(coefs[0:6], nx, ny, e)
        right = side_flux(coefs[6:12], nx, ny, e)
        for v in range(variables):
            left_ref[v * 2 * layers : (v + 1) * 2 * layers, lanes] = left[v] + bound * e[v]
            right_ref[v * 2 * layers : (v + 1) * 2 * layers, lanes] = right[v] - bound * e[v]
    left, right = left_ref[...], right_ref[...]
    near = scatter(left, hot_ref, 0) + scatter(right, hot_ref, 1)
    cut = scatter(right, hot_ref, 2)
    for v in range(variables):
        at = v * 2 * layers
        part = to_tiles(near[at : at + layers] + cut[at + layers : at + 2 * layers], tiles)
        p_ref[v * rows : (v + 1) * rows, :] = part
        s_ref[v * rows : (v + 1) * rows, :] = part * limiter_ref[v * rows : (v + 1) * rows, :]


def slope_kernel(layers, tiles, variables, vectors, with_gram, x_ref, a_ref, b_ref, c_ref, flux_ref,
                 where_ref, hot_ref, p_ref, v_ref, low_ref, high_ref, diag_ref, couple_ref, krylov_ref, *rest):
    finished = rest[:vectors]
    rest = rest[vectors:]
    if with_gram:
        gram_ref, *rest = rest
    w_ref, dots_ref, moved_ref, sums_ref = rest
    rows = layers * tiles
    size = variables * rows
    refs = ((x_ref, 0), (a_ref, 0), (b_ref, 0), (b_ref, size), (c_ref, 0))
    pieces = doubled(refs, layers, tiles, variables)
    faces = flux_ref.shape[2]
    for f in range(faces // LANES):
        lanes = slice(f * LANES, (f + 1) * LANES)
        e = gather_jump(pieces, where_ref, layers, tiles, variables, f)
        slope = flux_ref[15, :, lanes]
        for v in range(variables):
            moved_ref[v * 2 * layers : (v + 1) * 2 * layers, lanes] = slope * e[v]
    moved = moved_ref[...]
    own = scatter(moved, hot_ref, 1) - scatter(moved, hot_ref, 0)
    cut = scatter(moved, hot_ref, 2)
    layer = lax.broadcasted_iota(jnp.int32, (rows, LANES), 0) % layers
    total = []
    for v in range(variables):
        at = v * 2 * layers
        part = slice(v * rows, (v + 1) * rows)
        slope_part = to_tiles(own[at : at + layers] + cut[at + layers : at + 2 * layers], tiles)
        value = v_ref[part, :]
        low = pltpu.roll(low_ref[part, :], rows - (layers - 1), axis=0)
        high = pltpu.roll(high_ref[part, :], layers - 1, axis=0)
        above = jnp.where(layer == layers - 1, high, pltpu.roll(value, rows - 1, axis=0))
        below = jnp.where(layer == 0, low, pltpu.roll(value, 1, axis=0))
        out = diag_ref[...] * value + couple_ref[...] * (2.0 * value - above - below)
        out = out + p_ref[part, :] + slope_part
        w_ref[part, :] = out
        total.append(out)
    sums_ref[...] = jnp.zeros_like(sums_ref)
    basis = krylov_ref.shape[0] // size

    def put(at, ref, base):
        acc = None
        for v in range(variables):
            term = ref[base + v * rows : base + (v + 1) * rows, :] * total[v]
            acc = term if acc is None else acc + term
        sums_ref[at : at + 1, :] = jnp.sum(acc, axis=0, keepdims=True)

    for i in range(basis):
        put(i, krylov_ref, i * size)
    for j in range(vectors):
        put(basis + j, finished[j], 0)
    put(basis + PRODUCTS, w_ref, 0)
    dots = lax.dot_general(
        jnp.ones((8, LANES), jnp.float32), sums_ref[...], NT,
        precision=lax.Precision.HIGHEST, preferred_element_type=jnp.float32,
    )
    if with_gram:
        message = gram_ref[...]
        message = jnp.concatenate([message[0:1] + dots[0:1], message[1:]], axis=0)
        dots_ref[...] = jnp.broadcast_to(message[None], dots_ref.shape)
    else:
        dots_ref[...] = jnp.broadcast_to(dots[0:1], dots_ref.shape)


def inverse_of(packed, basis, per_row, scratch_ref):
    height = scratch_ref.shape[0]
    lane = lax.broadcasted_iota(jnp.int32, (height, LANES), 1)
    row = lax.broadcasted_iota(jnp.int32, (height, LANES), 0)
    scratch_ref[...] = jnp.zeros_like(scratch_ref)
    for i in range(basis):
        at = DOT_LANES + (i % per_row) * basis
        scratch_ref[i : i + 1, 0:basis] = packed[i // per_row : i // per_row + 1, at : at + basis]
    work = scratch_ref[...] + jnp.where(jnp.logical_and(lane == row + basis, row < basis), 1.0, 0.0)
    for k in range(basis):
        pivot_row = work[k : k + 1, :]
        scaled = pivot_row / pivot_row[:, k : k + 1]
        column = jnp.where(row == k, 0.0, jnp.broadcast_to(work[:, k : k + 1], work.shape))
        work = jnp.where(row == k, scaled, work - column * scaled)
    moved = pltpu.roll(work, LANES - basis, axis=1)
    return jnp.where(lane < basis, moved, 0.0)


def update_kernel(count_all, size, vectors, with_gram, per_row, got_ref, w_ref, krylov_ref, *rest):
    finished = rest[:vectors]
    rest = rest[vectors:]
    if with_gram:
        next_ref, hess_ref, inverse_ref, scratch_ref = rest
    else:
        inverse_ref, next_ref, hess_ref = rest
    basis = krylov_ref.shape[0] // size
    scale = 1.0 / count_all
    if with_gram:
        packed = jnp.sum(got_ref[...], axis=0) * scale
        inverse = inverse_of(packed, basis, per_row, scratch_ref)
        inverse_ref[...] = inverse
        p = packed[0:1, :]
    else:
        p = jnp.sum(got_ref[...], axis=0, keepdims=True) * scale
        inverse = inverse_ref[...]
    lane = lax.broadcasted_iota(jnp.int32, (1, LANES), 1)
    square = jnp.sum(jnp.where(lane == basis + PRODUCTS, p, 0.0), axis=1, keepdims=True)
    wide = inverse.shape
    solved = jnp.broadcast_to(jnp.sum(inverse * p, axis=1, keepdims=True), wide)
    diagonal = lax.broadcasted_iota(jnp.int32, wide, 0) == lax.broadcasted_iota(jnp.int32, wide, 1)
    solved_row = jnp.sum(jnp.where(diagonal, solved, 0.0), axis=0, keepdims=True)
    column = jnp.where(lane < basis, solved_row, jnp.where(lane < basis + vectors, p, 0.0))
    norm = jnp.sqrt(square - jnp.sum(column * p, axis=1, keepdims=True) + EPSILON)
    hess_ref[...] = jnp.where(lane == basis + PRODUCTS - 1, norm, column)
    rest_of = w_ref[...]
    for i in range(basis):
        rest_of = rest_of - solved[i : i + 1, :] * krylov_ref[i * size : (i + 1) * size, :]
    for j in range(vectors):
        rest_of = rest_of - p[:, basis + j : basis + j + 1] * finished[j][...]
    next_ref[...] = rest_of / norm


def on_device(krylov, limiter, pseudo_diag, face_states, face_angle, face_area, slope_weight,
              span_coupling, face_cells, send_list, send_count):
    basis, variables, layers, cells = krylov.shape
    cap = send_list.shape[1]
    faces = face_cells.shape[1]
    tiles = cells // LANES
    rows = layers * tiles
    size = variables * rows
    dom_count = lax.axis_size("dom")
    span_count = lax.axis_size("span")
    devices = dom_count * span_count
    count_all = variables * layers * cells * devices
    bits = (cells - 1).bit_length()
    messages = 5 * layers + 4
    height = -(-basis // 8) * 8
    per_row = (LANES - DOT_LANES) // basis
    packed_rows = -(-basis // per_row)

    def in_rows(value):
        lead = value.shape[:-2]
        value = value.reshape(lead + (layers, tiles, LANES))
        return jnp.swapaxes(value, -3, -2).reshape(lead[:-1] + (-1, LANES) if lead else (rows, LANES))

    swap = [(i, i ^ 1) for i in range(dom_count)]
    hop = [(i, i + 2 - 4 * (i % 2)) for i in range(dom_count) if 0 <= i + 2 - 4 * (i % 2) < dom_count]

    def window(x):
        a = lax.ppermute(x, "dom", swap)
        b = lax.ppermute(jnp.concatenate([x, a], axis=0), "dom", hop)
        c = lax.ppermute(b[size:], "dom", swap)
        return a, b, c

    def layer_neighbours(x):
        up = [(i, (i + 1) % span_count) for i in range(span_count)]
        low = lax.ppermute(x, "span", up)
        if span_count == 2:
            return low, low
        return low, lax.ppermute(x, "span", [(t, s) for s, t in up])

    odd = (lax.axis_index("dom") % 2).astype(jnp.int32).reshape(1)
    as_row = lambda value: value.reshape(1, faces)
    coef, row, index, message = call(
        functools.partial(prepare_kernel, cells, cap, bits),
        (f32(9, layers, faces), f32(3, faces), i32(3, faces), f32(PEERS * messages, cap)),
        odd, face_states, as_row(jnp.cos(face_angle)), as_row(jnp.sin(face_angle)),
        as_row(face_area), as_row(slope_weight), face_cells, send_list, smem=(0,),
    )
    basis_rows = in_rows(krylov.reshape(basis * variables, layers, cells)).reshape(basis * size, LANES)
    current = basis_rows[(basis - 1) * size :]
    first = jnp.concatenate([current, message[messages:]], axis=0)
    a = lax.ppermute(first, "dom", swap)
    second = jnp.concatenate(
        [current, a[:size], message[:messages], a[size + messages :]], axis=0
    )
    b = lax.ppermute(second, "dom", hop)
    third = jnp.concatenate([b[size : 2 * size], b[2 * size + 2 * messages :]], axis=0)
    c = lax.ppermute(third, "dom", swap)
    window_now = (a, b, c)

    flux, where, hot = call(
        functools.partial(build_kernel, cells, cap, bits, layers),
        (
            f32(16, 2 * layers, faces),
            i32(2, 2 * layers, faces),
            jax.ShapeDtypeStruct((3, cells, faces), jnp.bfloat16),
        ),
        coef, row, index,
        b[2 * size : 2 * size + messages],
        b[2 * size + messages : 2 * size + 2 * messages],
        a[size : size + messages],
        c[size:],
    )

    gram = jnp.einsum("kvlc,jvlc->kj", krylov, krylov, precision=lax.Precision.HIGHEST)
    gram = jnp.pad(gram, ((0, packed_rows * per_row - basis), (0, 0)))
    gram = gram.reshape(packed_rows, per_row * basis)
    gram = jnp.pad(gram, ((0, 0), (DOT_LANES, LANES - DOT_LANES - per_row * basis)))
    limit_rows = in_rows(limiter)
    diag_rows = in_rows(pseudo_diag)
    couple_rows = jnp.repeat(span_coupling.reshape(tiles, LANES), layers, axis=0)

    vectors = []
    hess_rows = []
    inverse = None
    for number in range(PRODUCTS):
        low, high = layer_neighbours(current)
        state_part, slope_adj = call(
            functools.partial(state_kernel, layers, tiles, variables, (0, 0, 0, 0)),
            (f32(size, LANES), f32(size, LANES)),
            current, *window_now, flux, where, hot, limit_rows,
            scratch=[pltpu.VMEM((variables * 2 * layers, faces), jnp.float32)] * 2,
        )
        slope_window = window(slope_adj)
        with_gram = number == 0
        extra = [gram] if with_gram else []
        dots_shape = f32(devices, packed_rows, LANES) if with_gram else f32(devices, LANES)
        product, dots = call(
            functools.partial(slope_kernel, layers, tiles, variables, number, with_gram),
            (f32(size, LANES), dots_shape),
            slope_adj, *slope_window, flux, where, hot, state_part, current, low, high, diag_rows,
            couple_rows, basis_rows, *vectors, *extra,
            scratch=[
                pltpu.VMEM((variables * 2 * layers, faces), jnp.float32),
                pltpu.VMEM((LANES, LANES), jnp.float32),
            ],
        )
        got = lax.all_to_all(dots, ("span", "dom"), 0, 0, tiled=True)
        next_shapes = (f32(size, LANES), f32(1, LANES))
        update = functools.partial(update_kernel, count_all, size, number, with_gram, per_row)
        if with_gram:
            current, hess, inverse = call(
                update, next_shapes + (f32(height, LANES),), got, product, basis_rows,
                scratch=[pltpu.VMEM((height, LANES), jnp.float32)],
            )
        else:
            current, hess = call(update, next_shapes, got, product, basis_rows, *vectors, inverse)
        vectors.append(current)
        hess_rows.append(hess[:, : basis + PRODUCTS])
        if number + 1 < PRODUCTS:
            window_now = window(current)
    stacked = jnp.stack(vectors).reshape(PRODUCTS, variables, tiles, layers, LANES)
    stacked = jnp.swapaxes(stacked, 2, 3).reshape(PRODUCTS, variables, layers, cells)
    return (stacked, jnp.concatenate(hess_rows, axis=0))


def solution(mesh):
    return jax.shard_map(
        on_device,
        mesh=mesh,
        in_specs=(
            P(None, None, "span", "dom"),
            P(None, "span", "dom"),
            P("span", "dom"),
            P(None, None, "span", "dom"),
            P("dom"),
            P("dom"),
            P("dom"),
            P("dom"),
            P(None, "dom"),
            P(None, "dom"),
            P(None, "dom"),
        ),
        out_specs=(P(None, None, "span", "dom"), P()),
        check_vma=False,
    )
```

profile of v0, /device:TPU:0, one launch (start us, length us, event | category | flops | bytes accessed | tf_op | source)
XLA Modules:
  0.0 101.4 jit_solution(9318667048894831545)
XLA Ops:
  0.6 0.7 copy-done.8
  1.4 0.6 copy-done.7
  2.1 0.0 copy-done.6
  2.1 0.0 copy-done.4
  2.1 0.9 copy-done.2
  3.0 0.3 shard_map.113
  3.3 0.7 slice.80
  4.1 0.5 collective-permute-start
  4.6 0.9 collective-permute-done.a_ref
  5.5 4.8 %collective-permute-start.1 = (f32[152,128]{1,0:T(8,128)S(1)}, f32[152,128]{1,0:T(8,128)S(1)}, u32[]{:S(2)}, u32[]{:S(2)}) collective-permute-start(f32[152,128]{1,0:T(8,128)S(1)} %pad_maximum_fusion), channel_id=1, source_target_pairs={{0,2},{2,4},{3,1},{4,6},{5,3},{6,8},{7,5},{8,10},{9,7},{10,12},{11... | collective-permute-start | bytes 233480 | tf_op jit(solution)/shard_map/ppermute | solution.py:435
  10.2 2.7 %collective-permute-done.1.b_ref = f32[152,128]{1,0:T(8,128)S(1)} collective-permute-done((f32[152,128]{1,0:T(8,128)S(1)}, f32[152,128]{1,0:T(8,128)S(1)}, u32[]{:S(2)}, u32[]{:S(2)}) %collective-permute-start.1) | collective-permute-done | bytes 77856 | tf_op jit(solution)/shard_map/ppermute | solution.py:435
  13.0 0.1 collective-permute-start.2
  13.1 1.2 %collective-permute-done.2.c_ref = f32[64,128]{1,0:T(8,128)S(1)} collective-permute-done((f32[64,128]{1,0:T(8,128)S(1)}, f32[64,128]{1,0:T(8,128)S(1)}, u32[]{:S(2)}, u32[]{:S(2)}) %collective-permute-start.2) | collective-permute-done | bytes 32800 | tf_op jit(solution)/shard_map/ppermute | solution.py:437
  14.3 0.4 shard_map.114
  14.6 0.4 copy-done.1
  15.0 0.8 shard_map.115
  15.8 0.2 collective-permute-start.3
  16.1 1.0 %collective-permute-done.3.a_ref = f32[40,128]{1,0:T(8,128)S(1)} collective-permute-done((f32[40,128]{1,0:T(8,128)S(1)}, f32[40,128]{1,0:T(8,128)S(1)}, u32[]{:S(2)}, u32[]{:S(2)}) %collective-permute-start.3) | collective-permute-done | bytes 20512 | tf_op jit(solution)/shard_map/ppermute | solution.py:408
  17.1 4.4 %collective-permute-start.4 = (f32[80,128]{1,0:T(8,128)S(1)}, f32[80,128]{1,0:T(8,128)S(1)}, u32[]{:S(2)}, u32[]{:S(2)}) collective-permute-start(f32[80,128]{1,0:T(8,128)S(1)} %pad_maximum_fusion.2), channel_id=1, source_target_pairs={{0,2},{2,4},{3,1},{4,6},{5,3},{6,8},{7,5},{8,10},{9,7},{10,12},{11... | collective-permute-start | bytes 122888 | tf_op jit(solution)/shard_map/ppermute | solution.py:409
  21.5 1.6 %collective-permute-start.6 = (f32[40,128]{1,0:T(8,128)S(1)}, f32[40,128]{1,0:T(8,128)S(1)}, u32[]{:S(2)}, u32[]{:S(2)}) collective-permute-start(f32[40,128]{1,0:T(8,128)S(1)} %bitcast.57), channel_id=1, source_target_pairs={{0,16},{16,0},{1,17},{17,1},{2,18},{18,2},{3,19},{19,3},{4,20},{20... | collective-permute-start | bytes 61448 | tf_op jit(solution)/shard_map/ppermute | solution.py:415
  23.0 0.4 collective-permute-done.4.b_ref
  23.5 0.6 convolution_bitcast_fusion
  24.1 0.1 reshape.70
  24.2 0.1 pad.4.rest_0_
  24.3 1.1 %collective-permute-done.6.low_ref.high_ref = f32[40,128]{1,0:T(8,128)S(1)} collective-permute-done((f32[40,128]{1,0:T(8,128)S(1)}, f32[40,128]{1,0:T(8,128)S(1)}, u32[]{:S(2)}, u32[]{:S(2)}) %collective-permute-start.6) | collective-permute-done | bytes 20512 | tf_op jit(solution)/shard_map/ppermute | solution.py:415
  25.3 0.7 copy-done.9
  26.0 0.7 copy-done.3
  26.7 1.2 %shard_map.116 = (f32[40,128]{1,0:T(8,128)S(1)}, f32[32,4,128]{2,1,0:T(4,128)S(1)}) custom-call(f32[40,128]{1,0:T(8,128)S(1)} %get-tuple-element.35.x_ref, f32[40,128]{1,0:T(8,128)S(1)} %collective-permute-done.3.a_ref, f32[80,128]{1,0:T(8,128)S(1)} %collective-permute-done.4.b_ref, f32[40,128]{1,0:T(8,128)S(1)} %collective-permute-done.5.c_ref, ...), custom_call_target="tpu_custom_call" | custom-call | tf_op jit(solution)/shard_map/pallas_call | solution.py:30
  27.9 12.9 %all_to_all.27.got_ref = f32[32,4,128]{2,1,0:T(4,128)S(1)} all-to-all(f32[32,4,128]{2,1,0:T(4,128)S(1)} %get-tuple-element.37), channel_id=1, replica_groups=mesh['span'=2,'dom'=16] {'span','dom'}, dimensions={0} | all-to-all | bytes 131072 | tf_op jit(solution)/shard_map/all_to_all | solution.py:487
  40.8 1.9 %shard_map.117 = (f32[40,128]{1,0:T(8,128)S(1)}, f32[1,128]{1,0:T(1,128)S(1)}, f32[24,128]{1,0:T(8,128)S(1)}) custom-call(f32[32,4,128]{2,1,0:T(4,128)S(1)} %all_to_all.27.got_ref, f32[40,128]{1,0:T(8,128)S(1)} %get-tuple-element.38.w_ref, f32[800,128]{1,0:T(8,128)S(1)} %bitcast.47), custom_call_target="tpu_custom_call" | custom-call | tf_op jit(solution)/shard_map/pallas_call | solution.py:30
  42.7 0.2 collective-permute-start.7
  42.9 1.1 %collective-permute-done.7.a_ref = f32[40,128]{1,0:T(8,128)S(1)} collective-permute-done((f32[40,128]{1,0:T(8,128)S(1)}, f32[40,128]{1,0:T(8,128)S(1)}, u32[]{:S(2)}, u32[]{:S(2)}) %collective-permute-start.7) | collective-permute-done | bytes 20512 | tf_op jit(solution)/shard_map/ppermute | solution.py:408
  44.0 2.3 %collective-permute-start.8 = (f32[80,128]{1,0:T(8,128)S(1)}, f32[80,128]{1,0:T(8,128)S(1)}, u32[]{:S(2)}, u32[]{:S(2)}) collective-permute-start(f32[80,128]{1,0:T(8,128)S(1)} %pad_maximum_fusion.3), channel_id=1, source_target_pairs={{0,2},{2,4},{3,1},{4,6},{5,3},{6,8},{7,5},{8,10},{9,7},{10,12},{11... | collective-permute-start | bytes 122888 | tf_op jit(solution)/shard_map/ppermute | solution.py:409
  46.3 2.0 %collective-permute-done.8.b_ref = f32[80,128]{1,0:T(8,128)S(1)} collective-permute-done((f32[80,128]{1,0:T(8,128)S(1)}, f32[80,128]{1,0:T(8,128)S(1)}, u32[]{:S(2)}, u32[]{:S(2)}) %collective-permute-start.8) | collective-permute-done | bytes 40992 | tf_op jit(solution)/shard_map/ppermute | solution.py:409
  48.3 0.6 collective-permute-start.9
  48.9 0.8 collective-permute-done.9.c_ref
  49.7 0.8 shard_map.118
  50.6 0.4 collective-permute-start.10
  51.0 0.8 collective-permute-done.10.a_ref
  51.8 4.1 %collective-permute-start.11 = (f32[80,128]{1,0:T(8,128)S(1)}, f32[80,128]{1,0:T(8,128)S(1)}, u32[]{:S(2)}, u32[]{:S(2)}) collective-permute-start(f32[80,128]{1,0:T(8,128)S(1)} %pad_maximum_fusion.4), channel_id=1, source_target_pairs={{0,2},{2,4},{3,1},{4,6},{5,3},{6,8},{7,5},{8,10},{9,7},{10,12},{11... | collective-permute-start | bytes 122888 | tf_op jit(solution)/shard_map/ppermute | solution.py:409
  56.0 0.7 collective-permute-start.13
  56.7 1.3 %collective-permute-done.11.b_ref = f32[80,128]{1,0:T(8,128)S(1)} collective-permute-done((f32[80,128]{1,0:T(8,128)S(1)}, f32[80,128]{1,0:T(8,128)S(1)}, u32[]{:S(2)}, u32[]{:S(2)}) %collective-permute-start.11) | collective-permute-done | bytes 40992 | tf_op jit(solution)/shard_map/ppermute | solution.py:409
  57.9 1.9 %collective-permute-done.13.low_ref.high_ref = f32[40,128]{1,0:T(8,128)S(1)} collective-permute-done((f32[40,128]{1,0:T(8,128)S(1)}, f32[40,128]{1,0:T(8,128)S(1)}, u32[]{:S(2)}, u32[]{:S(2)}) %collective-permute-start.13) | collective-permute-done | bytes 20512 | tf_op jit(solution)/shard_map/ppermute | solution.py:415
  59.8 1.2 %shard_map.119 = (f32[40,128]{1,0:T(8,128)S(1)}, f32[32,128]{1,0:T(8,128)S(1)}) custom-call(f32[40,128]{1,0:T(8,128)S(1)} %get-tuple-element.40.x_ref, f32[40,128]{1,0:T(8,128)S(1)} %collective-permute-done.10.a_ref, f32[80,128]{1,0:T(8,128)S(1)} %collective-permute-done.11.b_ref, f32[40,128]{1,0:T(8,128)S(1)} %collective-permute-done.12.c_ref, ...), custom_call_target="tpu_custom_call" | custom-call | tf_op jit(solution)/shard_map/pallas_call | solution.py:30
  61.0 10.3 %all_to_all.28 = f32[32,1,128]{2,1,0:T(1,128)S(1)} all-to-all(f32[32,1,128]{2,1,0:T(1,128)S(1)} %bitcast.72), channel_id=1, replica_groups=mesh['span'=2,'dom'=16] {'span','dom'}, dimensions={0} | all-to-all | bytes 32768 | tf_op jit(solution)/shard_map/all_to_all | solution.py:487
  71.3 0.2 shard_map.120
  71.5 0.1 collective-permute-start.14
  71.5 1.2 %collective-permute-done.14.a_ref = f32[40,128]{1,0:T(8,128)S(1)} collective-permute-done((f32[40,128]{1,0:T(8,128)S(1)}, f32[40,128]{1,0:T(8,128)S(1)}, u32[]{:S(2)}, u32[]{:S(2)}) %collective-permute-start.14) | collective-permute-done | bytes 20512 | tf_op jit(solution)/shard_map/ppermute | solution.py:408
  72.7 2.4 %collective-permute-start.15 = (f32[80,128]{1,0:T(8,128)S(1)}, f32[80,128]{1,0:T(8,128)S(1)}, u32[]{:S(2)}, u32[]{:S(2)}) collective-permute-start(f32[80,128]{1,0:T(8,128)S(1)} %pad_maximum_fusion.5), channel_id=1, source_target_pairs={{0,2},{2,4},{3,1},{4,6},{5,3},{6,8},{7,5},{8,10},{9,7},{10,12},{11... | collective-permute-start | bytes 122888 | tf_op jit(solution)/shard_map/ppermute | solution.py:409
  75.2 2.0 %collective-permute-done.15.b_ref = f32[80,128]{1,0:T(8,128)S(1)} collective-permute-done((f32[80,128]{1,0:T(8,128)S(1)}, f32[80,128]{1,0:T(8,128)S(1)}, u32[]{:S(2)}, u32[]{:S(2)}) %collective-permute-start.15) | collective-permute-done | bytes 40992 | tf_op jit(solution)/shard_map/ppermute | solution.py:409
  77.1 0.5 collective-permute-start.16
  77.6 0.8 collective-permute-done.16.c_ref
  78.5 0.8 shard_map.121
  79.3 0.4 collective-permute-start.17
  79.7 0.8 collective-permute-done.17.a_ref
  80.6 4.2 %collective-permute-start.18 = (f32[80,128]{1,0:T(8,128)S(1)}, f32[80,128]{1,0:T(8,128)S(1)}, u32[]{:S(2)}, u32[]{:S(2)}) collective-permute-start(f32[80,128]{1,0:T(8,128)S(1)} %pad_maximum_fusion.6), channel_id=1, source_target_pairs={{0,2},{2,4},{3,1},{4,6},{5,3},{6,8},{7,5},{8,10},{9,7},{10,12},{11... | collective-permute-start | bytes 122888 | tf_op jit(solution)/shard_map/ppermute | solution.py:409
  84.8 0.7 collective-permute-start.20
  85.4 1.3 %collective-permute-done.18.b_ref = f32[80,128]{1,0:T(8,128)S(1)} collective-permute-done((f32[80,128]{1,0:T(8,128)S(1)}, f32[80,128]{1,0:T(8,128)S(1)}, u32[]{:S(2)}, u32[]{:S(2)}) %collective-permute-start.18) | collective-permute-done | bytes 40992 | tf_op jit(solution)/shard_map/ppermute | solution.py:409
  86.8 1.9 %collective-permute-done.20.low_ref.high_ref = f32[40,128]{1,0:T(8,128)S(1)} collective-permute-done((f32[40,128]{1,0:T(8,128)S(1)}, f32[40,128]{1,0:T(8,128)S(1)}, u32[]{:S(2)}, u32[]{:S(2)}) %collective-permute-start.20) | collective-permute-done | bytes 20512 | tf_op jit(solution)/shard_map/ppermute | solution.py:415
  88.6 1.2 %shard_map.122 = (f32[40,128]{1,0:T(8,128)S(1)}, f32[32,128]{1,0:T(8,128)S(1)}) custom-call(f32[40,128]{1,0:T(8,128)S(1)} %get-tuple-element.46.x_ref, f32[40,128]{1,0:T(8,128)S(1)} %collective-permute-done.17.a_ref, f32[80,128]{1,0:T(8,128)S(1)} %collective-permute-done.18.b_ref, f32[40,128]{1,0:T(8,128)S(1)} %collective-permute-done.19.c_ref, ...), custom_call_target="tpu_custom_call" | custom-call | tf_op jit(solution)/shard_map/pallas_call | solution.py:30
  89.8 10.1 %all_to_all.29 = f32[32,1,128]{2,1,0:T(1,128)S(1)} all-to-all(f32[32,1,128]{2,1,0:T(1,128)S(1)} %bitcast.71), channel_id=1, replica_groups=mesh['span'=2,'dom'=16] {'span','dom'}, dimensions={0} | all-to-all | bytes 32768 | tf_op jit(solution)/shard_map/all_to_all | solution.py:487
  99.9 0.2 shard_map.123
  100.1 0.6 pad_maximum_fusion.8
  100.7 0.6 maximum_bitcast_fusion
  (41 shorter events, 0.2 us)
Async XLA Ops:
  0.6 0.7 copy-start.8
  1.4 0.7 copy-start.7
  1.4 0.7 copy-start.6
  1.4 0.7 copy-start.4
  1.4 0.7 copy-start.5
  2.1 0.9 copy-start.2
  4.1 1.4 %collective-permute-start = (f32[112,128]{1,0:T(8,128)S(1)}, f32[112,128]{1,0:T(8,128)S(1)}, u32[]{:S(2)}, u32[]{:S(2)}) collective-permute-start(f32[112,128]{1,0:T(8,128)S(1)} %pad_maximum_fusion.1), channel_id=1, source_target_pairs={{0,1},{1,0},{2,3},{3,2},{4,5},{5,4},{6,7},{7,6},{8,9},{9,8},{10,11... | collective-permute-start | bytes 172040 | tf_op jit(solution)/shard_map/ppermute | solution.py:431
  5.5 7.5 %collective-permute-start.1 = (f32[152,128]{1,0:T(8,128)S(1)}, f32[152,128]{1,0:T(8,128)S(1)}, u32[]{:S(2)}, u32[]{:S(2)}) collective-permute-start(f32[152,128]{1,0:T(8,128)S(1)} %pad_maximum_fusion), channel_id=1, source_target_pairs={{0,2},{2,4},{3,1},{4,6},{5,3},{6,8},{7,5},{8,10},{9,7},{10,12},{11... | collective-permute-start | bytes 233480 | tf_op jit(solution)/shard_map/ppermute | solution.py:435
  13.0 1.3 %collective-permute-start.2 = (f32[64,128]{1,0:T(8,128)S(1)}, f32[64,128]{1,0:T(8,128)S(1)}, u32[]{:S(2)}, u32[]{:S(2)}) collective-permute-start(f32[64,128]{1,0:T(8,128)S(1)} %pad_maximum_fusion.7), channel_id=1, source_target_pairs={{0,1},{1,0},{2,3},{3,2},{4,5},{5,4},{6,7},{7,6},{8,9},{9,8},{10,11... | collective-permute-start | bytes 98312 | tf_op jit(solution)/shard_map/ppermute | solution.py:437
  14.3 0.7 copy-start.1
  15.0 8.5 %copy-start = (f32[20,5,4,256]{3,2,1,0:T(4,128)S(1)}, f32[20,5,4,256]{3,2,1,0:T(4,128)}, u32[]{:S(2)}) copy-start(f32[20,5,4,256]{3,2,1,0:T(4,128)} %param.11) | copy-start | bytes 1228804
  15.8 1.3 %collective-permute-start.3 = (f32[40,128]{1,0:T(8,128)S(1)}, f32[40,128]{1,0:T(8,128)S(1)}, u32[]{:S(2)}, u32[]{:S(2)}) collective-permute-start(f32[40,128]{1,0:T(8,128)S(1)} %get-tuple-element.35.x_ref), channel_id=1, source_target_pairs={{0,1},{1,0},{2,3},{3,2},{4,5},{5,4},{6,7},{7,6},{8,9},{9,8},{10,11... | collective-permute-start | bytes 61448 | tf_op jit(solution)/shard_map/ppermute | solution.py:408
  17.1 6.4 %collective-permute-start.4 = (f32[80,128]{1,0:T(8,128)S(1)}, f32[80,128]{1,0:T(8,128)S(1)}, u32[]{:S(2)}, u32[]{:S(2)}) collective-permute-start(f32[80,128]{1,0:T(8,128)S(1)} %pad_maximum_fusion.2), channel_id=1, source_target_pairs={{0,2},{2,4},{3,1},{4,6},{5,3},{6,8},{7,5},{8,10},{9,7},{10,12},{11... | collective-permute-start | bytes 122888 | tf_op jit(solution)/shard_map/ppermute | solution.py:409
  21.5 3.8 %collective-permute-start.6 = (f32[40,128]{1,0:T(8,128)S(1)}, f32[40,128]{1,0:T(8,128)S(1)}, u32[]{:S(2)}, u32[]{:S(2)}) collective-permute-start(f32[40,128]{1,0:T(8,128)S(1)} %bitcast.57), channel_id=1, source_target_pairs={{0,16},{16,0},{1,17},{17,1},{2,18},{18,2},{3,19},{19,3},{4,20},{20... | collective-permute-start | bytes 61448 | tf_op jit(solution)/shard_map/ppermute | solution.py:415
  23.5 1.9 %collective-permute-start.5 = (f32[40,128]{1,0:T(8,128)S(1)}, f32[40,128]{1,0:T(8,128)S(1)}, u32[]{:S(2)}, u32[]{:S(2)}) collective-permute-start(f32[40,128]{1,0:T(8,128)S(1)} %slice.89), channel_id=1, source_target_pairs={{0,1},{1,0},{2,3},{3,2},{4,5},{5,4},{6,7},{7,6},{8,9},{9,8},{10,11... | collective-permute-start | bytes 61448 | tf_op jit(solution)/shard_map/ppermute | solution.py:410
  25.3 0.7 copy-start.9
  26.0 0.7 copy-start.3
  42.7 1.3 %collective-permute-start.7 = (f32[40,128]{1,0:T(8,128)S(1)}, f32[40,128]{1,0:T(8,128)S(1)}, u32[]{:S(2)}, u32[]{:S(2)}) collective-permute-start(f32[40,128]{1,0:T(8,128)S(1)} %get-tuple-element.39.x_ref.v_ref.rest_0_), channel_id=1, source_target_pairs={{0,1},{1,0},{2,3},{3,2},{4,5},{5,4},{6,7},{7,6},{8,9},{9,8},{10,11... | collective-permute-start | bytes 61448 | tf_op jit(solution)/shard_map/ppermute | solution.py:408
  44.0 4.3 %collective-permute-start.8 = (f32[80,128]{1,0:T(8,128)S(1)}, f32[80,128]{1,0:T(8,128)S(1)}, u32[]{:S(2)}, u32[]{:S(2)}) collective-permute-start(f32[80,128]{1,0:T(8,128)S(1)} %pad_maximum_fusion.3), channel_id=1, source_target_pairs={{0,2},{2,4},{3,1},{4,6},{5,3},{6,8},{7,5},{8,10},{9,7},{10,12},{11... | collective-permute-start | bytes 122888 | tf_op jit(solution)/shard_map/ppermute | solution.py:409
  48.3 1.4 %collective-permute-start.9 = (f32[40,128]{1,0:T(8,128)S(1)}, f32[40,128]{1,0:T(8,128)S(1)}, u32[]{:S(2)}, u32[]{:S(2)}) collective-permute-start(f32[40,128]{1,0:T(8,128)S(1)} %slice.90), channel_id=1, source_target_pairs={{0,1},{1,0},{2,3},{3,2},{4,5},{5,4},{6,7},{7,6},{8,9},{9,8},{10,11... | collective-permute-start | bytes 61448 | tf_op jit(solution)/shard_map/ppermute | solution.py:410
  50.6 1.3 %collective-permute-start.10 = (f32[40,128]{1,0:T(8,128)S(1)}, f32[40,128]{1,0:T(8,128)S(1)}, u32[]{:S(2)}, u32[]{:S(2)}) collective-permute-start(f32[40,128]{1,0:T(8,128)S(1)} %get-tuple-element.40.x_ref), channel_id=1, source_target_pairs={{0,1},{1,0},{2,3},{3,2},{4,5},{5,4},{6,7},{7,6},{8,9},{9,8},{10,11... | collective-permute-start | bytes 61448 | tf_op jit(solution)/shard_map/ppermute | solution.py:408
  51.8 6.1 %collective-permute-start.11 = (f32[80,128]{1,0:T(8,128)S(1)}, f32[80,128]{1,0:T(8,128)S(1)}, u32[]{:S(2)}, u32[]{:S(2)}) collective-permute-start(f32[80,128]{1,0:T(8,128)S(1)} %pad_maximum_fusion.4), channel_id=1, source_target_pairs={{0,2},{2,4},{3,1},{4,6},{5,3},{6,8},{7,5},{8,10},{9,7},{10,12},{11... | collective-permute-start | bytes 122888 | tf_op jit(solution)/shard_map/ppermute | solution.py:409
  56.0 3.8 %collective-permute-start.13 = (f32[40,128]{1,0:T(8,128)S(1)}, f32[40,128]{1,0:T(8,128)S(1)}, u32[]{:S(2)}, u32[]{:S(2)}) collective-permute-start(f32[40,128]{1,0:T(8,128)S(1)} %get-tuple-element.39.x_ref.v_ref.rest_0_), channel_id=1, source_target_pairs={{0,16},{16,0},{1,17},{17,1},{2,18},{18,2},{3,19},{19,3},{4,20},{20... | collective-permute-start | bytes 61448 | tf_op jit(solution)/shard_map/ppermute | solution.py:415
  57.9 1.9 %collective-permute-start.12 = (f32[40,128]{1,0:T(8,128)S(1)}, f32[40,128]{1,0:T(8,128)S(1)}, u32[]{:S(2)}, u32[]{:S(2)}) collective-permute-start(f32[40,128]{1,0:T(8,128)S(1)} %slice.91), channel_id=1, source_target_pairs={{0,1},{1,0},{2,3},{3,2},{4,5},{5,4},{6,7},{7,6},{8,9},{9,8},{10,11... | collective-permute-start | bytes 61448 | tf_op jit(solution)/shard_map/ppermute | solution.py:410
  71.5 1.2 %collective-permute-start.14 = (f32[40,128]{1,0:T(8,128)S(1)}, f32[40,128]{1,0:T(8,128)S(1)}, u32[]{:S(2)}, u32[]{:S(2)}) collective-permute-start(f32[40,128]{1,0:T(8,128)S(1)} %get-tuple-element.45.x_ref.v_ref.rest_1_), channel_id=1, source_target_pairs={{0,1},{1,0},{2,3},{3,2},{4,5},{5,4},{6,7},{7,6},{8,9},{9,8},{10,11... | collective-permute-start | bytes 61448 | tf_op jit(solution)/shard_map/ppermute | solution.py:408
  72.7 4.4 %collective-permute-start.15 = (f32[80,128]{1,0:T(8,128)S(1)}, f32[80,128]{1,0:T(8,128)S(1)}, u32[]{:S(2)}, u32[]{:S(2)}) collective-permute-start(f32[80,128]{1,0:T(8,128)S(1)} %pad_maximum_fusion.5), channel_id=1, source_target_pairs={{0,2},{2,4},{3,1},{4,6},{5,3},{6,8},{7,5},{8,10},{9,7},{10,12},{11... | collective-permute-start | bytes 122888 | tf_op jit(solution)/shard_map/ppermute | solution.py:409
  77.1 1.3 %collective-permute-start.16 = (f32[40,128]{1,0:T(8,128)S(1)}, f32[40,128]{1,0:T(8,128)S(1)}, u32[]{:S(2)}, u32[]{:S(2)}) collective-permute-start(f32[40,128]{1,0:T(8,128)S(1)} %slice.92), channel_id=1, source_target_pairs={{0,1},{1,0},{2,3},{3,2},{4,5},{5,4},{6,7},{7,6},{8,9},{9,8},{10,11... | collective-permute-start | bytes 61448 | tf_op jit(solution)/shard_map/ppermute | solution.py:410
  79.3 1.3 %collective-permute-start.17 = (f32[40,128]{1,0:T(8,128)S(1)}, f32[40,128]{1,0:T(8,128)S(1)}, u32[]{:S(2)}, u32[]{:S(2)}) collective-permute-start(f32[40,128]{1,0:T(8,128)S(1)} %get-tuple-element.46.x_ref), channel_id=1, source_target_pairs={{0,1},{1,0},{2,3},{3,2},{4,5},{5,4},{6,7},{7,6},{8,9},{9,8},{10,11... | collective-permute-start | bytes 61448 | tf_op jit(solution)/shard_map/ppermute | solution.py:408
  80.6 6.2 %collective-permute-start.18 = (f32[80,128]{1,0:T(8,128)S(1)}, f32[80,128]{1,0:T(8,128)S(1)}, u32[]{:S(2)}, u32[]{:S(2)}) collective-permute-start(f32[80,128]{1,0:T(8,128)S(1)} %pad_maximum_fusion.6), channel_id=1, source_target_pairs={{0,2},{2,4},{3,1},{4,6},{5,3},{6,8},{7,5},{8,10},{9,7},{10,12},{11... | collective-permute-start | bytes 122888 | tf_op jit(solution)/shard_map/ppermute | solution.py:409
  84.8 3.8 %collective-permute-start.20 = (f32[40,128]{1,0:T(8,128)S(1)}, f32[40,128]{1,0:T(8,128)S(1)}, u32[]{:S(2)}, u32[]{:S(2)}) collective-permute-start(f32[40,128]{1,0:T(8,128)S(1)} %get-tuple-element.45.x_ref.v_ref.rest_1_), channel_id=1, source_target_pairs={{0,16},{16,0},{1,17},{17,1},{2,18},{18,2},{3,19},{19,3},{4,20},{20... | collective-permute-start | bytes 61448 | tf_op jit(solution)/shard_map/ppermute | solution.py:415
  86.8 1.9 %collective-permute-start.19 = (f32[40,128]{1,0:T(8,128)S(1)}, f32[40,128]{1,0:T(8,128)S(1)}, u32[]{:S(2)}, u32[]{:S(2)}) collective-permute-start(f32[40,128]{1,0:T(8,128)S(1)} %slice.93), channel_id=1, source_target_pairs={{0,1},{1,0},{2,3},{3,2},{4,5},{5,4},{6,7},{7,6},{8,9},{9,8},{10,11... | collective-permute-start | bytes 61448 | tf_op jit(solution)/shard_map/ppermute | solution.py:410
where the time goes:
time: 102 us; the launch traced here: 101 us
  blocking collectives  33.3 us (33%)
  starting transfers between devices  28.1 us (28%)
  waiting for transfers between devices  23.2 us (23%)
  Pallas kernels  9.04 us (9%)
  local copies, waits for them, and re-layouts  4.96 us (5%)
  other arithmetic  1.27 us (1%)
    all_to_all x3, blocking collectives, on_device(): got = lax.all_to_all(dots, ('span', 'dom'), 0, 0, tiled=True)  33.3 us
    ppermute x5, starting transfers between devices, window(): b = lax.ppermute(jnp.concatenate([x, a], axis=0), 'dom', hop)  17.5 us
    pallas_call x11, Pallas kernels, call(): pl.pallas_call(kernel, out_shape=out_shape, in_specs=specs, out_specs=out...  9.04 us
    ppermute x5, waiting for transfers between devices, window(): b = lax.ppermute(jnp.concatenate([x, a], axis=0), 'dom', hop)  6.94 us
    ppermute x5, waiting for transfers between devices, window(): a = lax.ppermute(x, 'dom', swap)  4.97 us
    ppermute x3, waiting for transfers between devices, layer_neighbours(): low = lax.ppermute(x, 'span', up)  4.81 us
    ppermute x1, starting transfers between devices, on_device(): b = lax.ppermute(second, 'dom', hop)  4.76 us
    unnamed x20, local copies, waits for them, and re-layouts  3.99 us
  transfers between devices with their start and end apart: 21, of which 18 were waited for; matrix products, arithmetic and copies ran while one was open for 1% of the time, Pallas kernels for 0%

commit v1 on v0

--- a/solution.py
+++ b/solution.py
@@ -402,7 +402,10 @@
         return jnp.swapaxes(value, -3, -2).reshape(lead[:-1] + (-1, LANES) if lead else (rows, LANES))
 
     swap = [(i, i ^ 1) for i in range(dom_count)]
-    hop = [(i, i + 2 - 4 * (i % 2)) for i in range(dom_count) if 0 <= i + 2 - 4 * (i % 2) < dom_count]
+    hop = [(i, i + 2 if i + 2 < dom_count else i + 1) for i in range(0, dom_count, 2)]
+    hop += [(i, i - 2 if i >= 2 else i - 1) for i in range(1, dom_count, 2)]
+    place = lax.axis_index("dom")
+    outside = jnp.logical_or(place == 0, place == dom_count - 1)
 
     def window(x):
         a = lax.ppermute(x, "dom", swap)
@@ -433,7 +436,8 @@
         [current, a[:size], message[:messages], a[size + messages :]], axis=0
     )
     b = lax.ppermute(second, "dom", hop)
-    third = jnp.concatenate([b[size : 2 * size], b[2 * size + 2 * messages :]], axis=0)
+    got_messages = jnp.where(outside, 0.0, b[2 * size :])
+    third = jnp.concatenate([b[size : 2 * size], got_messages[2 * messages :]], axis=0)
     c = lax.ppermute(third, "dom", swap)
     window_now = (a, b, c)
 
@@ -445,8 +449,8 @@
             jax.ShapeDtypeStruct((3, cells, faces), jnp.bfloat16),
         ),
         coef, row, index,
-        b[2 * size : 2 * size + messages],
-        b[2 * size + messages : 2 * size + 2 * messages],
+        got_messages[:messages],
+        got_messages[messages : 2 * messages],
         a[size : size + messages],
         c[size:],
     )

time: 102 us -> 90.6 us (0.89)
  starting transfers between devices: 28.1 us -> 16.5 us
    ppermute x5, starting transfers between devices: 17.5 us -> 8 us  [window(): b = lax.ppermute(jnp.concatenate([x, a], axis=0), 'dom', hop)]
    ppermute x1, starting transfers between devices: 4.76 us -> 2.91 us  [on_device(): b = lax.ppermute(second, 'dom', hop)]
where the time goes in v1:
time: 90.6 us; the launch traced here: 90.1 us
  blocking collectives  33.6 us (37%)
  waiting for transfers between devices  23.3 us (26%)
  starting transfers between devices  16.5 us (18%)
  Pallas kernels  9.04 us (10%)
  local copies, waits for them, and re-layouts  4.97 us (5%)
  other arithmetic  1.28 us (1%)
    all_to_all x3, blocking collectives, on_device(): got = lax.all_to_all(dots, ('span', 'dom'), 0, 0, tiled=True)  33.6 us
    pallas_call x11, Pallas kernels, call(): pl.pallas_call(kernel, out_shape=out_shape, in_specs=specs, out_specs=out...  9.04 us
    ppermute x5, starting transfers between devices, window(): b = lax.ppermute(jnp.concatenate([x, a], axis=0), 'dom', hop)  8 us
    ppermute x5, waiting for transfers between devices, window(): b = lax.ppermute(jnp.concatenate([x, a], axis=0), 'dom', hop)  7.24 us
    ppermute x5, waiting for transfers between devices, window(): a = lax.ppermute(x, 'dom', swap)  4.97 us
    ppermute x3, waiting for transfers between devices, layer_neighbours(): low = lax.ppermute(x, 'span', up)  4.55 us
    unnamed x20, local copies, waits for them, and re-layouts  3.99 us
    ppermute x1, starting transfers between devices, on_device(): b = lax.ppermute(second, 'dom', hop)  2.91 us
  transfers between devices with their start and end apart: 21, of which 18 were waited for; matrix products, arithmetic and copies ran while one was open for 1% of the time, Pallas kernels for 0%

profile of v1, /device:TPU:0, one launch (start us, length us, event | category | flops | bytes accessed | tf_op | source)
XLA Modules:
  0.0 90.1 jit_solution(10495875085452244689)
XLA Ops:
  0.6 0.7 copy-done.8
  1.4 0.6 copy-done.7
  2.1 0.0 copy-done.6
  2.1 0.0 copy-done.4
  2.1 0.9 copy-done.2
  3.0 0.3 shard_map.113
  3.3 0.7 slice.84
  4.1 0.5 collective-permute-start
  4.6 0.9 collective-permute-done.a_ref
  5.5 2.9 %collective-permute-start.1 = (f32[152,128]{1,0:T(8,128)S(1)}, f32[152,128]{1,0:T(8,128)S(1)}, u32[]{:S(2)}, u32[]{:S(2)}) collective-permute-start(f32[152,128]{1,0:T(8,128)S(1)} %pad_maximum_fusion), channel_id=1, source_target_pairs={{0,2},{2,4},{4,6},{6,8},{8,10},{10,12},{12,14},{14,15},{1,0},{3,1}... | collective-permute-start | bytes 233480 | tf_op jit(solution)/shard_map/ppermute | solution.py:438
  8.4 2.7 %collective-permute-done.1.b_ref = f32[152,128]{1,0:T(8,128)S(1)} collective-permute-done((f32[152,128]{1,0:T(8,128)S(1)}, f32[152,128]{1,0:T(8,128)S(1)}, u32[]{:S(2)}, u32[]{:S(2)}) %collective-permute-start.1) | collective-permute-done | bytes 77856 | tf_op jit(solution)/shard_map/ppermute | solution.py:438
  11.2 0.1 collective-permute-start.2
  11.3 1.2 %collective-permute-done.2.c_ref = f32[64,128]{1,0:T(8,128)S(1)} collective-permute-done((f32[64,128]{1,0:T(8,128)S(1)}, f32[64,128]{1,0:T(8,128)S(1)}, u32[]{:S(2)}, u32[]{:S(2)}) %collective-permute-start.2) | collective-permute-done | bytes 32800 | tf_op jit(solution)/shard_map/ppermute | solution.py:441
  12.5 0.4 shard_map.114
  12.8 0.4 copy-done.1
  13.2 0.8 shard_map.115
  14.0 0.2 collective-permute-start.3
  14.3 1.0 %collective-permute-done.3.a_ref = f32[40,128]{1,0:T(8,128)S(1)} collective-permute-done((f32[40,128]{1,0:T(8,128)S(1)}, f32[40,128]{1,0:T(8,128)S(1)}, u32[]{:S(2)}, u32[]{:S(2)}) %collective-permute-start.3) | collective-permute-done | bytes 20512 | tf_op jit(solution)/shard_map/ppermute | solution.py:411
  15.3 2.5 %collective-permute-start.4 = (f32[80,128]{1,0:T(8,128)S(1)}, f32[80,128]{1,0:T(8,128)S(1)}, u32[]{:S(2)}, u32[]{:S(2)}) collective-permute-start(f32[80,128]{1,0:T(8,128)S(1)} %pad_maximum_fusion.2), channel_id=1, source_target_pairs={{0,2},{2,4},{4,6},{6,8},{8,10},{10,12},{12,14},{14,15},{1,0},{3,1}... | collective-permute-start | bytes 122888 | tf_op jit(solution)/shard_map/ppermute | solution.py:412
  17.8 1.5 %collective-permute-start.6 = (f32[40,128]{1,0:T(8,128)S(1)}, f32[40,128]{1,0:T(8,128)S(1)}, u32[]{:S(2)}, u32[]{:S(2)}) collective-permute-start(f32[40,128]{1,0:T(8,128)S(1)} %bitcast.57), channel_id=1, source_target_pairs={{0,16},{16,0},{1,17},{17,1},{2,18},{18,2},{3,19},{19,3},{4,20},{20... | collective-permute-start | bytes 61448 | tf_op jit(solution)/shard_map/ppermute | solution.py:418
  19.3 0.5 collective-permute-done.4.b_ref
  19.8 0.6 convolution_bitcast_fusion
  20.4 0.1 reshape.70
  20.5 0.1 pad.4.rest_0_
  20.6 1.0 %collective-permute-done.6.low_ref.high_ref = f32[40,128]{1,0:T(8,128)S(1)} collective-permute-done((f32[40,128]{1,0:T(8,128)S(1)}, f32[40,128]{1,0:T(8,128)S(1)}, u32[]{:S(2)}, u32[]{:S(2)}) %collective-permute-start.6) | collective-permute-done | bytes 20512 | tf_op jit(solution)/shard_map/ppermute | solution.py:418
  21.6 0.7 copy-done.9
  22.2 0.7 copy-done.3
  22.9 1.2 %shard_map.116 = (f32[40,128]{1,0:T(8,128)S(1)}, f32[32,4,128]{2,1,0:T(4,128)S(1)}) custom-call(f32[40,128]{1,0:T(8,128)S(1)} %get-tuple-element.35.x_ref, f32[40,128]{1,0:T(8,128)S(1)} %collective-permute-done.3.a_ref, f32[80,128]{1,0:T(8,128)S(1)} %collective-permute-done.4.b_ref, f32[40,128]{1,0:T(8,128)S(1)} %collective-permute-done.5.c_ref, ...), custom_call_target="tpu_custom_call" | custom-call | tf_op jit(solution)/shard_map/pallas_call | solution.py:30
  24.1 13.0 %all_to_all.27.got_ref = f32[32,4,128]{2,1,0:T(4,128)S(1)} all-to-all(f32[32,4,128]{2,1,0:T(4,128)S(1)} %get-tuple-element.37), channel_id=1, replica_groups=mesh['span'=2,'dom'=16] {'span','dom'}, dimensions={0} | all-to-all | bytes 131072 | tf_op jit(solution)/shard_map/all_to_all | solution.py:491
  37.1 1.9 %shard_map.117 = (f32[40,128]{1,0:T(8,128)S(1)}, f32[1,128]{1,0:T(1,128)S(1)}, f32[24,128]{1,0:T(8,128)S(1)}) custom-call(f32[32,4,128]{2,1,0:T(4,128)S(1)} %all_to_all.27.got_ref, f32[40,128]{1,0:T(8,128)S(1)} %get-tuple-element.38.w_ref, f32[800,128]{1,0:T(8,128)S(1)} %bitcast.47), custom_call_target="tpu_custom_call" | custom-call | tf_op jit(solution)/shard_map/pallas_call | solution.py:30
  39.0 0.2 collective-permute-start.7
  39.2 1.1 %collective-permute-done.7.a_ref = f32[40,128]{1,0:T(8,128)S(1)} collective-permute-done((f32[40,128]{1,0:T(8,128)S(1)}, f32[40,128]{1,0:T(8,128)S(1)}, u32[]{:S(2)}, u32[]{:S(2)}) %collective-permute-start.7) | collective-permute-done | bytes 20512 | tf_op jit(solution)/shard_map/ppermute | solution.py:411
  40.3 0.5 collective-permute-start.8
  40.7 2.0 %collective-permute-done.8.b_ref = f32[80,128]{1,0:T(8,128)S(1)} collective-permute-done((f32[80,128]{1,0:T(8,128)S(1)}, f32[80,128]{1,0:T(8,128)S(1)}, u32[]{:S(2)}, u32[]{:S(2)}) %collective-permute-start.8) | collective-permute-done | bytes 40992 | tf_op jit(solution)/shard_map/ppermute | solution.py:412
  42.7 0.6 collective-permute-start.9
  43.3 0.8 collective-permute-done.9.c_ref
  44.2 0.8 shard_map.118
  45.0 0.4 collective-permute-start.10
  45.4 0.8 collective-permute-done.10.a_ref
  46.3 2.2 %collective-permute-start.11 = (f32[80,128]{1,0:T(8,128)S(1)}, f32[80,128]{1,0:T(8,128)S(1)}, u32[]{:S(2)}, u32[]{:S(2)}) collective-permute-start(f32[80,128]{1,0:T(8,128)S(1)} %pad_maximum_fusion.4), channel_id=1, source_target_pairs={{0,2},{2,4},{4,6},{6,8},{8,10},{10,12},{12,14},{14,15},{1,0},{3,1}... | collective-permute-start | bytes 122888 | tf_op jit(solution)/shard_map/ppermute | solution.py:412
  48.5 0.7 collective-permute-start.13
  49.1 1.3 %collective-permute-done.11.b_ref = f32[80,128]{1,0:T(8,128)S(1)} collective-permute-done((f32[80,128]{1,0:T(8,128)S(1)}, f32[80,128]{1,0:T(8,128)S(1)}, u32[]{:S(2)}, u32[]{:S(2)}) %collective-permute-start.11) | collective-permute-done | bytes 40992 | tf_op jit(solution)/shard_map/ppermute | solution.py:412
  50.5 1.8 %collective-permute-done.13.low_ref.high_ref = f32[40,128]{1,0:T(8,128)S(1)} collective-permute-done((f32[40,128]{1,0:T(8,128)S(1)}, f32[40,128]{1,0:T(8,128)S(1)}, u32[]{:S(2)}, u32[]{:S(2)}) %collective-permute-start.13) | collective-permute-done | bytes 20512 | tf_op jit(solution)/shard_map/ppermute | solution.py:418
  52.3 1.2 %shard_map.119 = (f32[40,128]{1,0:T(8,128)S(1)}, f32[32,128]{1,0:T(8,128)S(1)}) custom-call(f32[40,128]{1,0:T(8,128)S(1)} %get-tuple-element.40.x_ref, f32[40,128]{1,0:T(8,128)S(1)} %collective-permute-done.10.a_ref, f32[80,128]{1,0:T(8,128)S(1)} %collective-permute-done.11.b_ref, f32[40,128]{1,0:T(8,128)S(1)} %collective-permute-done.12.c_ref, ...), custom_call_target="tpu_custom_call" | custom-call | tf_op jit(solution)/shard_map/pallas_call | solution.py:30
  53.4 10.4 %all_to_all.28 = f32[32,1,128]{2,1,0:T(1,128)S(1)} all-to-all(f32[32,1,128]{2,1,0:T(1,128)S(1)} %bitcast.72), channel_id=1, replica_groups=mesh['span'=2,'dom'=16] {'span','dom'}, dimensions={0} | all-to-all | bytes 32768 | tf_op jit(solution)/shard_map/all_to_all | solution.py:491
  63.8 0.2 shard_map.120
  64.0 0.1 collective-permute-start.14
  64.1 1.2 %collective-permute-done.14.a_ref = f32[40,128]{1,0:T(8,128)S(1)} collective-permute-done((f32[40,128]{1,0:T(8,128)S(1)}, f32[40,128]{1,0:T(8,128)S(1)}, u32[]{:S(2)}, u32[]{:S(2)}) %collective-permute-start.14) | collective-permute-done | bytes 20512 | tf_op jit(solution)/shard_map/ppermute | solution.py:411
  65.3 0.5 collective-permute-start.15
  65.8 2.0 %collective-permute-done.15.b_ref = f32[80,128]{1,0:T(8,128)S(1)} collective-permute-done((f32[80,128]{1,0:T(8,128)S(1)}, f32[80,128]{1,0:T(8,128)S(1)}, u32[]{:S(2)}, u32[]{:S(2)}) %collective-permute-start.15) | collective-permute-done | bytes 40992 | tf_op jit(solution)/shard_map/ppermute | solution.py:412
  67.8 0.5 collective-permute-start.16
  68.3 0.8 collective-permute-done.16.c_ref
  69.1 0.8 shard_map.121
  70.0 0.4 collective-permute-start.17
  70.4 0.8 collective-permute-done.17.a_ref
  71.2 2.3 %collective-permute-start.18 = (f32[80,128]{1,0:T(8,128)S(1)}, f32[80,128]{1,0:T(8,128)S(1)}, u32[]{:S(2)}, u32[]{:S(2)}) collective-permute-start(f32[80,128]{1,0:T(8,128)S(1)} %pad_maximum_fusion.6), channel_id=1, source_target_pairs={{0,2},{2,4},{4,6},{6,8},{8,10},{10,12},{12,14},{14,15},{1,0},{3,1}... | collective-permute-start | bytes 122888 | tf_op jit(solution)/shard_map/ppermute | solution.py:412
  73.5 0.6 collective-permute-start.20
  74.1 1.4 %collective-permute-done.18.b_ref = f32[80,128]{1,0:T(8,128)S(1)} collective-permute-done((f32[80,128]{1,0:T(8,128)S(1)}, f32[80,128]{1,0:T(8,128)S(1)}, u32[]{:S(2)}, u32[]{:S(2)}) %collective-permute-start.18) | collective-permute-done | bytes 40992 | tf_op jit(solution)/shard_map/ppermute | solution.py:412
  75.5 1.8 %collective-permute-done.20.low_ref.high_ref = f32[40,128]{1,0:T(8,128)S(1)} collective-permute-done((f32[40,128]{1,0:T(8,128)S(1)}, f32[40,128]{1,0:T(8,128)S(1)}, u32[]{:S(2)}, u32[]{:S(2)}) %collective-permute-start.20) | collective-permute-done | bytes 20512 | tf_op jit(solution)/shard_map/ppermute | solution.py:418
  77.3 1.2 %shard_map.122 = (f32[40,128]{1,0:T(8,128)S(1)}, f32[32,128]{1,0:T(8,128)S(1)}) custom-call(f32[40,128]{1,0:T(8,128)S(1)} %get-tuple-element.46.x_ref, f32[40,128]{1,0:T(8,128)S(1)} %collective-permute-done.17.a_ref, f32[80,128]{1,0:T(8,128)S(1)} %collective-permute-done.18.b_ref, f32[40,128]{1,0:T(8,128)S(1)} %collective-permute-done.19.c_ref, ...), custom_call_target="tpu_custom_call" | custom-call | tf_op jit(solution)/shard_map/pallas_call | solution.py:30
  78.5 10.2 %all_to_all.29 = f32[32,1,128]{2,1,0:T(1,128)S(1)} all-to-all(f32[32,1,128]{2,1,0:T(1,128)S(1)} %bitcast.71), channel_id=1, replica_groups=mesh['span'=2,'dom'=16] {'span','dom'}, dimensions={0} | all-to-all | bytes 32768 | tf_op jit(solution)/shard_map/all_to_all | solution.py:491
  88.7 0.2 shard_map.123
  88.9 0.6 pad_maximum_fusion.8
  89.5 0.6 maximum_bitcast_fusion
  (42 shorter events, 0.2 us)
Async XLA Ops:
  0.6 0.7 copy-start.8
  1.4 0.7 copy-start.7
  1.4 0.7 copy-start.6
  1.4 0.7 copy-start.4
  1.4 0.7 copy-start.5
  2.1 0.9 copy-start.2
  4.1 1.4 %collective-permute-start = (f32[112,128]{1,0:T(8,128)S(1)}, f32[112,128]{1,0:T(8,128)S(1)}, u32[]{:S(2)}, u32[]{:S(2)}) collective-permute-start(f32[112,128]{1,0:T(8,128)S(1)} %pad_maximum_fusion.1), channel_id=1, source_target_pairs={{0,1},{1,0},{2,3},{3,2},{4,5},{5,4},{6,7},{7,6},{8,9},{9,8},{10,11... | collective-permute-start | bytes 172040 | tf_op jit(solution)/shard_map/ppermute | solution.py:434
  5.5 5.7 %collective-permute-start.1 = (f32[152,128]{1,0:T(8,128)S(1)}, f32[152,128]{1,0:T(8,128)S(1)}, u32[]{:S(2)}, u32[]{:S(2)}) collective-permute-start(f32[152,128]{1,0:T(8,128)S(1)} %pad_maximum_fusion), channel_id=1, source_target_pairs={{0,2},{2,4},{4,6},{6,8},{8,10},{10,12},{12,14},{14,15},{1,0},{3,1}... | collective-permute-start | bytes 233480 | tf_op jit(solution)/shard_map/ppermute | solution.py:438
  11.2 1.3 %collective-permute-start.2 = (f32[64,128]{1,0:T(8,128)S(1)}, f32[64,128]{1,0:T(8,128)S(1)}, u32[]{:S(2)}, u32[]{:S(2)}) collective-permute-start(f32[64,128]{1,0:T(8,128)S(1)} %pad_maximum_fusion.7), channel_id=1, source_target_pairs={{0,1},{1,0},{2,3},{3,2},{4,5},{5,4},{6,7},{7,6},{8,9},{9,8},{10,11... | collective-permute-start | bytes 98312 | tf_op jit(solution)/shard_map/ppermute | solution.py:441
  12.5 0.7 copy-start.1
  13.2 6.6 %copy-start = (f32[20,5,4,256]{3,2,1,0:T(4,128)S(1)}, f32[20,5,4,256]{3,2,1,0:T(4,128)}, u32[]{:S(2)}) copy-start(f32[20,5,4,256]{3,2,1,0:T(4,128)} %param.11) | copy-start | bytes 1228804
  14.0 1.3 %collective-permute-start.3 = (f32[40,128]{1,0:T(8,128)S(1)}, f32[40,128]{1,0:T(8,128)S(1)}, u32[]{:S(2)}, u32[]{:S(2)}) collective-permute-start(f32[40,128]{1,0:T(8,128)S(1)} %get-tuple-element.35.x_ref), channel_id=1, source_target_pairs={{0,1},{1,0},{2,3},{3,2},{4,5},{5,4},{6,7},{7,6},{8,9},{9,8},{10,11... | collective-permute-start | bytes 61448 | tf_op jit(solution)/shard_map/ppermute | solution.py:411
  15.3 4.5 %collective-permute-start.4 = (f32[80,128]{1,0:T(8,128)S(1)}, f32[80,128]{1,0:T(8,128)S(1)}, u32[]{:S(2)}, u32[]{:S(2)}) collective-permute-start(f32[80,128]{1,0:T(8,128)S(1)} %pad_maximum_fusion.2), channel_id=1, source_target_pairs={{0,2},{2,4},{4,6},{6,8},{8,10},{10,12},{12,14},{14,15},{1,0},{3,1}... | collective-permute-start | bytes 122888 | tf_op jit(solution)/shard_map/ppermute | solution.py:412
  17.8 3.8 %collective-permute-start.6 = (f32[40,128]{1,0:T(8,128)S(1)}, f32[40,128]{1,0:T(8,128)S(1)}, u32[]{:S(2)}, u32[]{:S(2)}) collective-permute-start(f32[40,128]{1,0:T(8,128)S(1)} %bitcast.57), channel_id=1, source_target_pairs={{0,16},{16,0},{1,17},{17,1},{2,18},{18,2},{3,19},{19,3},{4,20},{20... | collective-permute-start | bytes 61448 | tf_op jit(solution)/shard_map/ppermute | solution.py:418
  19.8 1.8 %collective-permute-start.5 = (f32[40,128]{1,0:T(8,128)S(1)}, f32[40,128]{1,0:T(8,128)S(1)}, u32[]{:S(2)}, u32[]{:S(2)}) collective-permute-start(f32[40,128]{1,0:T(8,128)S(1)} %slice.94), channel_id=1, source_target_pairs={{0,1},{1,0},{2,3},{3,2},{4,5},{5,4},{6,7},{7,6},{8,9},{9,8},{10,11... | collective-permute-start | bytes 61448 | tf_op jit(solution)/shard_map/ppermute | solution.py:413
  21.6 0.7 copy-start.9
  22.2 0.7 copy-start.3
  39.0 1.3 %collective-permute-start.7 = (f32[40,128]{1,0:T(8,128)S(1)}, f32[40,128]{1,0:T(8,128)S(1)}, u32[]{:S(2)}, u32[]{:S(2)}) collective-permute-start(f32[40,128]{1,0:T(8,128)S(1)} %get-tuple-element.39.x_ref.v_ref.rest_0_), channel_id=1, source_target_pairs={{0,1},{1,0},{2,3},{3,2},{4,5},{5,4},{6,7},{7,6},{8,9},{9,8},{10,11... | collective-permute-start | bytes 61448 | tf_op jit(solution)/shard_map/ppermute | solution.py:411
  40.3 2.4 %collective-permute-start.8 = (f32[80,128]{1,0:T(8,128)S(1)}, f32[80,128]{1,0:T(8,128)S(1)}, u32[]{:S(2)}, u32[]{:S(2)}) collective-permute-start(f32[80,128]{1,0:T(8,128)S(1)} %pad_maximum_fusion.3), channel_id=1, source_target_pairs={{0,2},{2,4},{4,6},{6,8},{8,10},{10,12},{12,14},{14,15},{1,0},{3,1}... | collective-permute-start | bytes 122888 | tf_op jit(solution)/shard_map/ppermute | solution.py:412
  42.7 1.4 %collective-permute-start.9 = (f32[40,128]{1,0:T(8,128)S(1)}, f32[40,128]{1,0:T(8,128)S(1)}, u32[]{:S(2)}, u32[]{:S(2)}) collective-permute-start(f32[40,128]{1,0:T(8,128)S(1)} %slice.95), channel_id=1, source_target_pairs={{0,1},{1,0},{2,3},{3,2},{4,5},{5,4},{6,7},{7,6},{8,9},{9,8},{10,11... | collective-permute-start | bytes 61448 | tf_op jit(solution)/shard_map/ppermute | solution.py:413
  45.0 1.3 %collective-permute-start.10 = (f32[40,128]{1,0:T(8,128)S(1)}, f32[40,128]{1,0:T(8,128)S(1)}, u32[]{:S(2)}, u32[]{:S(2)}) collective-permute-start(f32[40,128]{1,0:T(8,128)S(1)} %get-tuple-element.40.x_ref), channel_id=1, source_target_pairs={{0,1},{1,0},{2,3},{3,2},{4,5},{5,4},{6,7},{7,6},{8,9},{9,8},{10,11... | collective-permute-start | bytes 61448 | tf_op jit(solution)/shard_map/ppermute | solution.py:411
  46.3 4.2 %collective-permute-start.11 = (f32[80,128]{1,0:T(8,128)S(1)}, f32[80,128]{1,0:T(8,128)S(1)}, u32[]{:S(2)}, u32[]{:S(2)}) collective-permute-start(f32[80,128]{1,0:T(8,128)S(1)} %pad_maximum_fusion.4), channel_id=1, source_target_pairs={{0,2},{2,4},{4,6},{6,8},{8,10},{10,12},{12,14},{14,15},{1,0},{3,1}... | collective-permute-start | bytes 122888 | tf_op jit(solution)/shard_map/ppermute | solution.py:412
  48.5 3.8 %collective-permute-start.13 = (f32[40,128]{1,0:T(8,128)S(1)}, f32[40,128]{1,0:T(8,128)S(1)}, u32[]{:S(2)}, u32[]{:S(2)}) collective-permute-start(f32[40,128]{1,0:T(8,128)S(1)} %get-tuple-element.39.x_ref.v_ref.rest_0_), channel_id=1, source_target_pairs={{0,16},{16,0},{1,17},{17,1},{2,18},{18,2},{3,19},{19,3},{4,20},{20... | collective-permute-start | bytes 61448 | tf_op jit(solution)/shard_map/ppermute | solution.py:418
  50.5 1.8 %collective-permute-start.12 = (f32[40,128]{1,0:T(8,128)S(1)}, f32[40,128]{1,0:T(8,128)S(1)}, u32[]{:S(2)}, u32[]{:S(2)}) collective-permute-start(f32[40,128]{1,0:T(8,128)S(1)} %slice.96), channel_id=1, source_target_pairs={{0,1},{1,0},{2,3},{3,2},{4,5},{5,4},{6,7},{7,6},{8,9},{9,8},{10,11... | collective-permute-start | bytes 61448 | tf_op jit(solution)/shard_map/ppermute | solution.py:413
  64.0 1.2 %collective-permute-start.14 = (f32[40,128]{1,0:T(8,128)S(1)}, f32[40,128]{1,0:T(8,128)S(1)}, u32[]{:S(2)}, u32[]{:S(2)}) collective-permute-start(f32[40,128]{1,0:T(8,128)S(1)} %get-tuple-element.45.x_ref.v_ref.rest_1_), channel_id=1, source_target_pairs={{0,1},{1,0},{2,3},{3,2},{4,5},{5,4},{6,7},{7,6},{8,9},{9,8},{10,11... | collective-permute-start | bytes 61448 | tf_op jit(solution)/shard_map/ppermute | solution.py:411
  65.3 2.5 %collective-permute-start.15 = (f32[80,128]{1,0:T(8,128)S(1)}, f32[80,128]{1,0:T(8,128)S(1)}, u32[]{:S(2)}, u32[]{:S(2)}) collective-permute-start(f32[80,128]{1,0:T(8,128)S(1)} %pad_maximum_fusion.5), channel_id=1, source_target_pairs={{0,2},{2,4},{4,6},{6,8},{8,10},{10,12},{12,14},{14,15},{1,0},{3,1}... | collective-permute-start | bytes 122888 | tf_op jit(solution)/shard_map/ppermute | solution.py:412
  67.8 1.3 %collective-permute-start.16 = (f32[40,128]{1,0:T(8,128)S(1)}, f32[40,128]{1,0:T(8,128)S(1)}, u32[]{:S(2)}, u32[]{:S(2)}) collective-permute-start(f32[40,128]{1,0:T(8,128)S(1)} %slice.97), channel_id=1, source_target_pairs={{0,1},{1,0},{2,3},{3,2},{4,5},{5,4},{6,7},{7,6},{8,9},{9,8},{10,11... | collective-permute-start | bytes 61448 | tf_op jit(solution)/shard_map/ppermute | solution.py:413
  70.0 1.3 %collective-permute-start.17 = (f32[40,128]{1,0:T(8,128)S(1)}, f32[40,128]{1,0:T(8,128)S(1)}, u32[]{:S(2)}, u32[]{:S(2)}) collective-permute-start(f32[40,128]{1,0:T(8,128)S(1)} %get-tuple-element.46.x_ref), channel_id=1, source_target_pairs={{0,1},{1,0},{2,3},{3,2},{4,5},{5,4},{6,7},{7,6},{8,9},{9,8},{10,11... | collective-permute-start | bytes 61448 | tf_op jit(solution)/shard_map/ppermute | solution.py:411
  71.2 4.3 %collective-permute-start.18 = (f32[80,128]{1,0:T(8,128)S(1)}, f32[80,128]{1,0:T(8,128)S(1)}, u32[]{:S(2)}, u32[]{:S(2)}) collective-permute-start(f32[80,128]{1,0:T(8,128)S(1)} %pad_maximum_fusion.6), channel_id=1, source_target_pairs={{0,2},{2,4},{4,6},{6,8},{8,10},{10,12},{12,14},{14,15},{1,0},{3,1}... | collective-permute-start | bytes 122888 | tf_op jit(solution)/shard_map/ppermute | solution.py:412
  73.5 3.8 %collective-permute-start.20 = (f32[40,128]{1,0:T(8,128)S(1)}, f32[40,128]{1,0:T(8,128)S(1)}, u32[]{:S(2)}, u32[]{:S(2)}) collective-permute-start(f32[40,128]{1,0:T(8,128)S(1)} %get-tuple-element.45.x_ref.v_ref.rest_1_), channel_id=1, source_target_pairs={{0,16},{16,0},{1,17},{17,1},{2,18},{18,2},{3,19},{19,3},{4,20},{20... | collective-permute-start | bytes 61448 | tf_op jit(solution)/shard_map/ppermute | solution.py:418
  75.5 1.8 %collective-permute-start.19 = (f32[40,128]{1,0:T(8,128)S(1)}, f32[40,128]{1,0:T(8,128)S(1)}, u32[]{:S(2)}, u32[]{:S(2)}) collective-permute-start(f32[40,128]{1,0:T(8,128)S(1)} %slice.98), channel_id=1, source_target_pairs={{0,1},{1,0},{2,3},{3,2},{4,5},{5,4},{6,7},{7,6},{8,9},{9,8},{10,11... | collective-permute-start | bytes 61448 | tf_op jit(solution)/shard_map/ppermute | solution.py:413

commit v2 on v0

v2 whole, which is shorter than its diff:
```python
import functools

import jax
import jax.numpy as jnp
from jax import lax
from jax.experimental import pallas as pl
from jax.experimental.pallas import tpu as pltpu
from jax.sharding import PartitionSpec as P

PRODUCTS = 3
PEERS = 4
EPSILON = 1e-06
GAMMA = 1.4
LANES = 128
DOT_LANES = 28

SENT_FACES = (((0, 0), (1, 1), (1, 0)), ((1, 3), (0, 2), (0, 3)))
SENT_LISTS = (((1, 3), (1, 2), (0, 3)), ((0, 0), (0, 1), (1, 0)))
HOLDER_BLOCK = ((0, 1, 1), (1, 0, 0))
NAMED_LIST = (((1, 3), (1, 2), (0, 3)), ((0, 0), (0, 1), (1, 0)))
GHOSTS = (
    ((1, 1, 0), (0, 1, None), (2, 0, 1), (2, 1, 2)),
    ((1, 0, 2), (1, 1, 1), (0, 0, None), (2, 0, 0)),
)
NAMING = (((0, 2), (1, 0), (1, 1)), ((0, 0), (0, 1), (1, 2)))

VMEM_LIMIT = 16 * 1024 * 1024
NT = (((1,), (1,)), ((), ()))


def call(kernel, out_shape, *args, smem=(), scratch=()):
    specs = [
        pl.BlockSpec(memory_space=pltpu.SMEM if i in smem else pltpu.VMEM)
        for i in range(len(args))
    ]
    out_specs = jax.tree.map(lambda _: pl.BlockSpec(memory_space=pltpu.VMEM), out_shape)
    return pl.pallas_call(
        kernel,
        out_shape=out_shape,
        in_specs=specs,
        out_specs=out_specs,
        scratch_shapes=list(scratch),
        compiler_params=pltpu.CompilerParams(vmem_limit_bytes=VMEM_LIMIT),
    )(*args)


def f32(*shape):
    return jax.ShapeDtypeStruct(shape, jnp.float32)


def i32(*shape):
    return jax.ShapeDtypeStruct(shape, jnp.int32)


def rows_of(shape):
    return lax.broadcasted_iota(jnp.int32, shape, 0)


def split_rows(value):
    high = value.astype(jnp.bfloat16).astype(jnp.float32)
    return jnp.concatenate([high, value - high], axis=0).astype(jnp.bfloat16)


def pair_swap(value, half):
    count = value.shape[0]
    first = (rows_of(value.shape) // half) % 2 == 0
    return jnp.where(first, pltpu.roll(value, count - half, axis=0), pltpu.roll(value, half, axis=0))


def mix(own, got, role, half):
    mine = (rows_of(own.shape) // half) % 2 == role
    return jnp.where(mine, own, pair_swap(got, half))


def take(source, index):
    return jnp.take_along_axis(source, index, axis=1, mode="promise_in_bounds")


def primitives(states, nx, ny):
    rho, mx, my, mz, energy = states
    inverse = 1.0 / rho
    ux, uy, uz = mx * inverse, my * inverse, mz * inverse
    pressure = (GAMMA - 1.0) * (energy - 0.5 * rho * (ux * ux + uy * uy + uz * uz))
    enthalpy = (energy + pressure) * inverse
    speed = jnp.abs(ux * nx + uy * ny) + jnp.sqrt(GAMMA * pressure * inverse)
    return [ux, uy, uz, enthalpy], speed


def side_terms(prims, nx, ny):
    ux, uy, uz, enthalpy = prims
    return [ux, uy, uz, enthalpy, ux * nx + uy * ny, 0.5 * (ux * ux + uy * uy + uz * uz)]


def spread(rows, each):
    return jnp.concatenate(
        [jnp.broadcast_to(rows[q : q + 1], (each, LANES)) for q in range(rows.shape[0])], axis=0
    )


def prepare_kernel(dims, at, place_ref, raw_ref, got_ref, flux_ref, index_ref, send_a_ref, send_b_ref,
                   value_ref, partner_ref, limiter_ref, diag_ref, couple_ref, pack_ref):
    cells, cap, bits, half, groups, size, variables, message = dims
    role, mirrored = place_ref[0], place_ref[1] == 1

    def own(name):
        start, count = at[name]
        return raw_ref[start : start + count, :], got_ref[start : start + count, :]

    def blocks(start, count):
        mine, other = raw_ref[start : start + count, :], got_ref[start : start + count, :]
        return jnp.where(role == 0, mine, other), jnp.where(role == 0, other, mine)

    mine, other = own("value")
    value = mix(mine, other, role, half)
    value_ref[...] = value
    partner_ref[...] = mix(other, mine, 1 - role, half)
    limiter_ref[...] = mix(*own("limiter"), role, half)
    diag_ref[...] = mix(*own("diag"), role, half)
    couple = blocks(*at["couple"])
    for t in range(cells // LANES):
        for b in range(2):
            row = (2 * t + b) * half
            couple_ref[row : row + half, :] = jnp.broadcast_to(couple[b][t : t + 1], (half, LANES))

    names = ("nx", "ny", "area", "slope", "owner", "other", "lists")
    plane = {name: blocks(*at[name]) for name in names}
    start = at["states"][0]
    picked, lists = [], []
    for b in range(2):
        states = []
        for k in range(2 * variables):
            both = blocks(start + k * groups * 2 * half, groups * 2 * half)[b]
            low = jnp.concatenate([both[2 * half * q : 2 * half * q + half] for q in range(groups)], axis=0)
            high = jnp.concatenate(
                [both[2 * half * q + half : 2 * half * (q + 1)] for q in range(groups)], axis=0
            )
            states.append(jnp.where(role == 0, low, high))
        nx, ny = spread(plane["nx"][b], half), spread(plane["ny"][b], half)
        scale = spread(0.5 * plane["area"][b], half)
        slope = spread(plane["slope"][b], half)
        left, speed_left = primitives(states[:variables], nx, ny)
        right, speed_right = primitives(states[variables:], nx, ny)
        bound = scale * jnp.maximum(speed_left, speed_right)
        nx, ny = nx * scale, ny * scale
        for k, term in enumerate(side_terms(left, nx, ny) + side_terms(right, nx, ny) + [bound, nx, ny, slope]):
            flux_ref[k, b] = term
        pack_ref[...] = jnp.zeros_like(pack_ref)
        for q in range(groups):
            lanes = slice(q * LANES, (q + 1) * LANES)
            for k, term in enumerate(right + [bound]):
                pack_ref[k * half : (k + 1) * half, lanes] = term[q * half : (q + 1) * half]
            scaled = 0.5 * plane["area"][b][q : q + 1]
            tail = [plane["nx"][b][q : q + 1] * scaled, plane["ny"][b][q : q + 1] * scaled]
            tail += [plane["slope"][b][q : q + 1], plane["owner"][b][q : q + 1]]
            for k, term in enumerate(tail):
                row = 5 * half + k
                pack_ref[row : row + 1, lanes] = term

        def line(rows):
            return jnp.concatenate([rows[q : q + 1] for q in range(rows.shape[0])], axis=1)

        owner = line(plane["owner"][b]).astype(jnp.int32)
        ghost = line(plane["other"][b]).astype(jnp.int32) - cells
        group = jnp.zeros_like(ghost)
        for g in range(1, PEERS):
            group = group + (ghost >= g * cap).astype(jnp.int32)
        flipped = ghost + (PEERS - 1 - 2 * group) * cap
        slot = jnp.where(jnp.logical_and(mirrored, ghost >= 0), flipped, ghost)
        plain = plane["lists"][b]
        turned = jnp.concatenate([plain[PEERS - 1 - g : PEERS - g] for g in range(PEERS)], axis=0)
        ordered = jnp.where(mirrored, turned, plain)
        lists.append(ordered)
        index_ref[3 * b : 3 * b + 1, :] = owner
        index_ref[3 * b + 1 : 3 * b + 2, :] = slot + cells
        index_ref[3 * b + 2 : 3 * b + 3, :] = line(ordered).astype(jnp.int32)
        faces = slot.shape[1]
        named = rows_of((PEERS * cap, faces)) == slot
        packed = pack_ref[...]
        result = lax.dot_general(
            split_rows(packed), named.astype(jnp.float32).astype(jnp.bfloat16), NT,
            preferred_element_type=jnp.float32,
        )
        picked.append(result[: packed.shape[0]] + result[packed.shape[0] :])
    for side, ref in enumerate((send_a_ref, send_b_ref)):
        ref[0:size, :] = value
        for g in range(3):
            b, j = SENT_FACES[side][g]
            part = picked[b][0:message, j * cap : (j + 1) * cap]
            b, j = SENT_LISTS[side][g]
            code = part[message - 1 :] * float(1 << bits) + lists[b][j : j + 1]
            row = size + g * message
            ref[row : row + message - 1, :] = part[: message - 1]
            ref[row + message - 1 : row + message, :] = code
        row = size + 3 * message
        ref[row:, :] = jnp.zeros((ref.shape[0] - row, LANES), jnp.float32)


def list_of(index_ref, b, j, cap):
    return index_ref[3 * b + 2 : 3 * b + 3, j * cap : (j + 1) * cap]


def hot_kernel(cells, cap, index_ref, hot_ref):
    faces = index_ref.shape[1]
    inside = []
    for b in range(2):
        local = index_ref[3 * b + 1 : 3 * b + 2, :]
        here = jnp.where(local < cells, local, -1)
        j = b + 1
        table = jnp.broadcast_to(list_of(index_ref, 1 - b, j, cap), (8, cap))
        parts = []
        for f in range(faces // LANES):
            slot = jnp.broadcast_to(local[:, f * LANES : (f + 1) * LANES], (8, LANES)) - cells - j * cap
            got = take(table, jnp.bitwise_and(slot, LANES - 1))
            ok = jnp.logical_and(slot >= 0, slot < cap)
            parts.append(jnp.where(ok, got, -1)[0:1])
        inside.append((here, jnp.concatenate(parts, axis=1)))
    owners = [index_ref[3 * b : 3 * b + 1, :] for b in range(2)]
    cut = []
    for b in range(2):
        pieces = []
        for side, g in NAMING[b]:
            block, j = NAMED_LIST[side][g]
            pieces.append(list_of(index_ref, block, j, cap))
        cut.append(pieces)
    lines = (
        jnp.concatenate(cut[0] + [owners[0], inside[0][0], inside[1][1]], axis=1),
        jnp.concatenate([inside[0][1], inside[1][0], owners[1]] + cut[1], axis=1),
    )
    for b in range(2):
        width = lines[b].shape[1]
        equal = rows_of((cells, width)) == lines[b]
        hot_ref[b] = jnp.where(equal, jnp.float32(1.0), 0.0).astype(jnp.bfloat16)


def build_kernel(cells, cap, bits, half, groups, message, index_ref, a_ref, b_ref, flux_ref, near_ref, far_ref):
    gots = (a_ref, b_ref)
    tiles = cells // LANES

    def stack(parts):
        count = sum(p.shape[0] for p in parts)
        tail = jnp.zeros((groups * half - count, LANES), parts[0].dtype)
        return jnp.concatenate(list(parts) + [tail], axis=0)

    codes = []
    for side, ref in enumerate(gots):
        def block(k):
            return stack([ref[g * message + k * half : g * message + (k + 1) * half, :] for g in range(3)])

        def line(k):
            row = 5 * half + k
            return stack(
                [jnp.broadcast_to(ref[g * message + row : g * message + row + 1, :], (half, LANES)) for g in range(3)]
            )

        nx, ny, slope = line(0), line(1), line(2)
        terms = side_terms([block(k) for k in range(4)], nx, ny) + [block(4), nx, ny, slope]
        for k, term in enumerate(terms):
            flux_ref[k, side] = term
        code = [ref[(g + 1) * message - 1 : (g + 1) * message, :].astype(jnp.int32) for g in range(3)]
        held = [jnp.broadcast_to(lax.shift_right_logical(c, bits), (half, LANES)) for c in code]
        near_ref[2 + side] = stack(held)
        mine = [
            jnp.broadcast_to(list_of(index_ref, *NAMED_LIST[side][g], cap), (half, LANES)) for g in range(3)
        ]
        far_ref[2 + side] = stack(mine)
        codes.append([jnp.bitwise_and(c, (1 << bits) - 1) for c in code])

    def place(cell, piece, block):
        tile = 2 * lax.shift_right_logical(cell, 7) + (2 * tiles * piece + block)
        return tile * LANES + jnp.bitwise_and(cell, LANES - 1)

    for b in range(2):
        owner = [index_ref[3 * b : 3 * b + 1, q * LANES : (q + 1) * LANES] for q in range(groups)]
        other = [index_ref[3 * b + 1 : 3 * b + 2, q * LANES : (q + 1) * LANES] for q in range(groups)]
        near_ref[b] = spread(jnp.concatenate(owner, axis=0), half)
        local = spread(jnp.concatenate(other, axis=0), half)
        value = place(local, 0, b)
        slot = local - cells
        low = jnp.bitwise_and(slot, LANES - 1)
        for j in range(PEERS):
            piece, block, g = GHOSTS[b][j]
            cell = list_of(index_ref, block, j, cap) if g is None else codes[piece - 1][g]
            table = jnp.broadcast_to(place(cell, piece, block), (groups * half, cap))
            inside = jnp.logical_and(slot >= j * cap, slot < (j + 1) * cap)
            value = jnp.where(inside, take(table, low), value)
        far_ref[b] = value


def tile_copies(refs, half, tiles, variables):
    rows = 2 * tiles * half
    row = rows_of((rows, LANES))
    pieces = []
    for ref in refs:
        piece = []
        for v in range(variables):
            value = ref[v * rows : (v + 1) * rows, :]
            parts = []
            for u in range(2 * tiles):
                part = value if u == 0 else pltpu.roll(value, rows - u * half, axis=0)
                width = half
                while width < rows:
                    part = jnp.where(row % (2 * width) < width, part, pltpu.roll(part, width, axis=0))
                    width *= 2
                parts.append(part)
            piece.append(parts)
        pieces.append(piece)
    return pieces


def jumps_of(pieces, near_ref, far_ref, half, tiles, variables, k):
    near, far = near_ref[k], far_ref[k]
    near_low, near_tile = jnp.bitwise_and(near, LANES - 1), lax.shift_right_logical(near, 7)
    far_low, far_tile = jnp.bitwise_and(far, LANES - 1), lax.shift_right_logical(far, 7)
    group = rows_of(near.shape) // half

    def mixed(piece, v, t, which):
        zero, one = pieces[piece][v][2 * t], pieces[piece][v][2 * t + 1]
        pick = jnp.zeros(near.shape, jnp.bool_)
        for g in range(3):
            if which[g]:
                pick = jnp.logical_or(pick, group == g)
        return jnp.where(pick, one, zero)

    jumps = []
    for v in range(variables):
        first, second = None, None
        for t in range(tiles):
            source = pieces[0][v][2 * t + k] if k < 2 else mixed(k - 1, v, t, HOLDER_BLOCK[k - 2])
            got = take(source, near_low)
            first = got if first is None else jnp.where(near_tile == t, got, first)
        if k < 2:
            for p in range(3):
                for u in range(2 * tiles):
                    got = take(pieces[p][v][u], far_low)
                    tile = 2 * tiles * p + u
                    second = got if second is None else jnp.where(far_tile == tile, got, second)
        else:
            blocks = [named[0] for named in NAMED_LIST[k - 2]]
            for t in range(tiles):
                got = take(mixed(0, v, t, blocks), far_low)
                second = got if second is None else jnp.where(far_tile == t, got, second)
        jumps.append(first - second)
    return jumps


def side_flux(coefs, nx, ny, e):
    ux, uy, uz, enthalpy, normal, kinetic = coefs
    alpha = ux * e[1] + uy * e[2] + uz * e[3] + enthalpy * e[4]
    beta = (GAMMA - 1.0) * (nx * e[1] + ny * e[2] + normal * e[4])
    total = e[0] + alpha
    return [
        beta * kinetic - alpha * normal,
        nx * total + normal * e[1] - beta * ux,
        ny * total + normal * e[2] - beta * uy,
        normal * e[3] - beta * uz,
        beta + normal * e[4],
    ]


def put_faces(terms_ref, base, half, groups, v, value):
    for q in range(groups):
        start = base + q * LANES
        terms_ref[v * half : (v + 1) * half, start : start + LANES] = value[q * half : (q + 1) * half]


def put_cut(terms_ref, cap, faces, half, side, v, value):
    for b in range(2):
        for n, (s, g) in enumerate(NAMING[b]):
            if s == side:
                start = n * cap + b * (3 * cap + 4 * faces)
                terms_ref[v * half : (v + 1) * half, start : start + cap] = value[g * half : (g + 1) * half]


def gathered(terms_ref, hot_ref, half, tiles, variables):
    width = hot_ref.shape[2]
    total = terms_ref.shape[1]
    results = []
    for b in range(2):
        value = terms_ref[:, 0:width] if b == 0 else terms_ref[:, total - width :]
        got = lax.dot_general(split_rows(value), hot_ref[b], NT, preferred_element_type=jnp.float32)
        count = got.shape[0] // 2
        results.append(got[:count] + got[count:])
    out = []
    for v in range(variables):
        parts = [
            results[b][v * half : (v + 1) * half, t * LANES : (t + 1) * LANES]
            for t in range(tiles)
            for b in range(2)
        ]
        out.append(jnp.concatenate(parts, axis=0))
    return out


def clear_tail(terms_ref, used):
    terms_ref[used:, :] = jnp.zeros((terms_ref.shape[0] - used, terms_ref.shape[1]), jnp.float32)


def state_kernel(cap, half, groups, tiles, variables, x_ref, a_ref, b_ref, flux_ref, cut_ref, near_ref, far_ref,
                 hot_ref, limiter_ref, p_ref, s_ref, terms_ref):
    rows = 2 * tiles * half
    faces = groups * LANES
    pieces = tile_copies((x_ref, a_ref, b_ref), half, tiles, variables)
    clear_tail(terms_ref, variables * half)
    for k in range(4):
        e = jumps_of(pieces, near_ref, far_ref, half, tiles, variables, k)
        if k < 2:
            coefs = [flux_ref[i, k] for i in range(15)]
            bound, nx, ny = coefs[12:]
            left = side_flux(coefs[0:6], nx, ny, e)
            right = side_flux(coefs[6:12], nx, ny, e)
            left_base = 3 * cap + (0 if k == 0 else 3 * faces)
            right_base = 3 * cap + (1 + k) * faces
            for v in range(variables):
                put_faces(terms_ref, left_base, half, groups, v, left[v] + bound * e[v])
                put_faces(terms_ref, right_base, half, groups, v, right[v] - bound * e[v])
        else:
            coefs = [cut_ref[i, k - 2] for i in range(9)]
            bound, nx, ny = coefs[6:]
            right = side_flux(coefs[0:6], nx, ny, e)
            for v in range(variables):
                put_cut(terms_ref, cap, faces, half, k - 2, v, right[v] - bound * e[v])
    for v, part in enumerate(gathered(terms_ref, hot_ref, half, tiles, variables)):
        p_ref[v * rows : (v + 1) * rows, :] = part
        s_ref[v * rows : (v + 1) * rows, :] = part * limiter_ref[v * rows : (v + 1) * rows, :]


def slope_kernel(cap, half, groups, tiles, variables, vectors, with_gram, place_ref, x_ref, a_ref, b_ref, flux_ref,
                 cut_ref, near_ref, far_ref, hot_ref, p_ref, v_ref, partner_ref, cross_ref, diag_ref, couple_ref,
                 krylov_ref, *rest):
    finished = rest[:vectors]
    rest = rest[vectors:]
    if with_gram:
        gram_ref, *rest = rest
    w_ref, dots_ref, terms_ref, sums_ref = rest
    rows = 2 * tiles * half
    size = variables * rows
    faces = groups * LANES
    role = place_ref[0]
    pieces = tile_copies((x_ref, a_ref, b_ref), half, tiles, variables)
    clear_tail(terms_ref, variables * half)
    for k in range(4):
        e = jumps_of(pieces, near_ref, far_ref, half, tiles, variables, k)
        if k < 2:
            slope = flux_ref[15, k]
            left_base = 3 * cap + (0 if k == 0 else 3 * faces)
            right_base = 3 * cap + (1 + k) * faces
            for v in range(variables):
                moved = slope * e[v]
                put_faces(terms_ref, left_base, half, groups, v, -moved)
                put_faces(terms_ref, right_base, half, groups, v, moved)
        else:
            slope = cut_ref[9, k - 2]
            for v in range(variables):
                put_cut(terms_ref, cap, faces, half, k - 2, v, slope * e[v])
    slope_parts = gathered(terms_ref, hot_ref, half, tiles, variables)
    layer = rows_of((rows, LANES)) % half
    total = []
    for v in range(variables):
        part = slice(v * rows, (v + 1) * rows)
        value = v_ref[part, :]
        partner, cross = partner_ref[part, :], cross_ref[part, :]
        high = pltpu.roll(jnp.where(role == 0, partner, cross), half - 1, axis=0)
        low = pltpu.roll(jnp.where(role == 0, cross, partner), rows - (half - 1), axis=0)
        above = jnp.where(layer == half - 1, high, pltpu.roll(value, rows - 1, axis=0))
        below = jnp.where(layer == 0, low, pltpu.roll(value, 1, axis=0))
        out = diag_ref[...] * value + couple_ref[...] * (2.0 * value - above - below)
        out = out + p_ref[part, :] + slope_parts[v]
        w_ref[part, :] = out
        total.append(out)
    sums_ref[...] = jnp.zeros_like(sums_ref)
    basis = krylov_ref.shape[0] // size

    def put(at, ref, base):
        acc = None
        for v in range(variables):
            term = ref[base + v * rows : base + (v + 1) * rows, :] * total[v]
            acc = term if acc is None else acc + term
        sums_ref[at : at + 1, :] = jnp.sum(acc, axis=0, keepdims=True)

    for i in range(basis):
        put(i, krylov_ref, i * size)
    for j in range(vectors):
        put(basis + j, finished[j], 0)
    put(basis + PRODUCTS, w_ref, 0)
    dots = lax.dot_general(
        jnp.ones((8, LANES), jnp.float32), sums_ref[...], NT,
        precision=lax.Precision.HIGHEST, preferred_element_type=jnp.float32,
    )
    if with_gram:
        message = gram_ref[...]
        message = jnp.concatenate([message[0:1] + dots[0:1], message[1:]], axis=0)
        dots_ref[...] = jnp.broadcast_to(message[None], dots_ref.shape)
    else:
        dots_ref[...] = jnp.broadcast_to(dots[0:1], dots_ref.shape)


def inverse_of(packed, basis, per_row, scratch_ref):
    height = scratch_ref.shape[0]
    lane = lax.broadcasted_iota(jnp.int32, (height, LANES), 1)
    row = rows_of((height, LANES))
    scratch_ref[...] = jnp.zeros_like(scratch_ref)
    for i in range(basis):
        at = DOT_LANES + (i % per_row) * basis
        scratch_ref[i : i + 1, 0:basis] = packed[i // per_row : i // per_row + 1, at : at + basis]
    work = scratch_ref[...] + jnp.where(jnp.logical_and(lane == row + basis, row < basis), 1.0, 0.0)
    for k in range(basis):
        pivot_row = work[k : k + 1, :]
        scaled = pivot_row / pivot_row[:, k : k + 1]
        column = jnp.where(row == k, 0.0, jnp.broadcast_to(work[:, k : k + 1], work.shape))
        work = jnp.where(row == k, scaled, work - column * scaled)
    moved = pltpu.roll(work, LANES - basis, axis=1)
    return jnp.where(lane < basis, moved, 0.0)


def mix_kernel(half, place_ref, own_ref, got_ref, out_ref):
    role = place_ref[0]
    out_ref[...] = mix(own_ref[...], got_ref[...], role, half)


def update_kernel(count_all, size, vectors, with_gram, per_row, got_ref, w_ref, krylov_ref, *rest):
    finished = rest[:vectors]
    rest = rest[vectors:]
    if with_gram:
        next_ref, hess_ref, inverse_ref, scratch_ref = rest
    else:
        inverse_ref, next_ref, hess_ref = rest
    basis = krylov_ref.shape[0] // size
    scale = 1.0 / count_all
    if with_gram:
        packed = jnp.sum(got_ref[...], axis=0) * scale
        inverse = inverse_of(packed, basis, per_row, scratch_ref)
        inverse_ref[...] = inverse
        p = packed[0:1, :]
    else:
        p = jnp.sum(got_ref[...], axis=0, keepdims=True) * scale
        inverse = inverse_ref[...]
    lane = lax.broadcasted_iota(jnp.int32, (1, LANES), 1)
    square = jnp.sum(jnp.where(lane == basis + PRODUCTS, p, 0.0), axis=1, keepdims=True)
    wide = inverse.shape
    solved = jnp.broadcast_to(jnp.sum(inverse * p, axis=1, keepdims=True), wide)
    diagonal = rows_of(wide) == lax.broadcasted_iota(jnp.int32, wide, 1)
    solved_row = jnp.sum(jnp.where(diagonal, solved, 0.0), axis=0, keepdims=True)
    column = jnp.where(lane < basis, solved_row, jnp.where(lane < basis + vectors, p, 0.0))
    norm = jnp.sqrt(square - jnp.sum(column * p, axis=1, keepdims=True) + EPSILON)
    hess_ref[...] = jnp.where(lane == basis + PRODUCTS - 1, norm, column)
    value = w_ref[...]
    for i in range(basis):
        value = value - solved[i : i + 1, :] * krylov_ref[i * size : (i + 1) * size, :]
    for j in range(vectors):
        value = value - p[:, basis + j : basis + j + 1] * finished[j][...]
    next_ref[...] = value / norm


def output_kernel(half, size, place_ref, *refs):
    out_ref = refs[-1]
    for m in range(PRODUCTS):
        out_ref[m * size : (m + 1) * size, :] = mix(refs[2 * m][...], refs[2 * m + 1][...], place_ref[0], half)


def on_device(krylov, limiter, pseudo_diag, face_states, face_angle, face_area, slope_weight,
              span_coupling, face_cells, send_list, send_count):
    basis, variables, layers, cells = krylov.shape
    cap = send_list.shape[1]
    faces = face_cells.shape[1]
    tiles = cells // LANES
    groups = faces // LANES
    half = layers // 2
    rows = layers * tiles
    size = variables * rows
    dom_count = lax.axis_size("dom")
    span_count = lax.axis_size("span")
    devices = dom_count * span_count
    count_all = variables * layers * cells * devices
    bits = (cells - 1).bit_length()
    message = 5 * half + 4
    height = -(-basis // 8) * 8
    per_row = (LANES - DOT_LANES) // basis
    packed_rows = -(-basis // per_row)

    def in_rows(value):
        width = value.shape[-1] // LANES
        value = value.reshape((-1, layers, width, LANES))
        return jnp.swapaxes(value, 1, 2).reshape(-1, LANES)

    block = lax.axis_index("dom")
    pair = block // 2
    mirrored = pair % 2
    role = (block + mirrored) % 2
    place = jnp.stack([role, mirrored]).astype(jnp.int32)
    at_end = jnp.logical_or(pair == 0, pair == dom_count // 2 - 1)

    swap = [(i, i ^ 1) for i in range(dom_count)]
    to_a = [(i, i ^ 3) for i in range(dom_count)]
    to_b = []
    for i in range(dom_count):
        other = ((i // 2 + 1) ^ 1) - 1
        to_b.append((i, 2 * other + 1 - i % 2 if 0 <= other < dom_count // 2 else i ^ 1))
    cross = []
    for s in range(span_count):
        for i in range(dom_count):
            step = 1 if (i + i // 2) % 2 else -1
            cross.append((s * dom_count + i, ((s + step) % span_count) * dom_count + (i ^ 1)))

    def send(x, pairs):
        return lax.ppermute(x, "dom", pairs)

    def neighbours(x):
        return send(x, to_a), send(x, to_b)

    def across(x):
        return lax.ppermute(x, ("span", "dom"), cross)

    basis_rows = in_rows(krylov)
    parts = {
        "value": basis_rows[(basis - 1) * size :],
        "limiter": in_rows(limiter),
        "diag": in_rows(pseudo_diag),
        "states": in_rows(face_states),
        "nx": jnp.cos(face_angle).reshape(groups, LANES),
        "ny": jnp.sin(face_angle).reshape(groups, LANES),
        "area": face_area.reshape(groups, LANES),
        "slope": slope_weight.reshape(groups, LANES),
        "owner": face_cells[0].astype(jnp.float32).reshape(groups, LANES),
        "other": face_cells[1].astype(jnp.float32).reshape(groups, LANES),
        "lists": send_list.astype(jnp.float32),
        "couple": span_coupling.reshape(tiles, LANES),
    }
    at, start = {}, 0
    for name, value in parts.items():
        at[name] = (start, value.shape[0])
        start += value.shape[0]
    raw = jnp.concatenate(list(parts.values()), axis=0)
    got_raw = send(raw, swap)
    sent_rows = -(-(size + 3 * message) // 8) * 8
    dims = (cells, cap, bits, half, groups, size, variables, message)
    (flux, index, send_a, send_b, current, partner, limit_rows, diag_rows, couple_rows) = call(
        functools.partial(prepare_kernel, dims, at),
        (
            f32(16, 2, groups * half, LANES), i32(6, faces), f32(sent_rows, LANES), f32(sent_rows, LANES),
            f32(size, LANES), f32(size, LANES), f32(size, LANES), f32(rows, LANES), f32(rows, LANES),
        ),
        place, raw, got_raw, smem=(0,),
        scratch=[pltpu.VMEM((-(-message // 8) * 8, faces), jnp.float32)],
    )
    got_a = send(send_a, to_a)
    got_b = send(send_b, to_b)
    message_b = jnp.where(at_end, 0.0, got_b[size:])
    hot_width = 3 * cap + 3 * faces
    hot = call(
        functools.partial(hot_kernel, cells, cap),
        jax.ShapeDtypeStruct((2, cells, hot_width), jnp.bfloat16),
        index,
    )
    cut, near, far = call(
        functools.partial(build_kernel, cells, cap, bits, half, groups, message),
        (
            f32(10, 2, groups * half, LANES), i32(4, groups * half, LANES), i32(4, groups * half, LANES),
        ),
        index, got_a[size:], message_b,
    )
    window = (got_a[:size], got_b[:size])

    mixed_rows = call(
        functools.partial(mix_kernel, half), f32(basis * size, LANES), place, basis_rows, send(basis_rows, swap),
        smem=(0,),
    )

    gram = jnp.einsum("kvlc,jvlc->kj", krylov, krylov, precision=lax.Precision.HIGHEST)
    gram = jnp.pad(gram, ((0, packed_rows * per_row - basis), (0, 0)))
    gram = gram.reshape(packed_rows, per_row * basis)
    gram = jnp.pad(gram, ((0, 0), (DOT_LANES, LANES - DOT_LANES - per_row * basis)))

    terms = pltpu.VMEM((-(-variables * half // 8) * 8, 6 * cap + 4 * faces), jnp.float32)
    vectors = []
    finished = []
    hess_rows = []
    inverse = None
    for number in range(PRODUCTS):
        crossed = across(current)
        state_part, slope_adj = call(
            functools.partial(state_kernel, cap, half, groups, tiles, variables),
            (f32(size, LANES), f32(size, LANES)),
            current, *window, flux, cut, near, far, hot, limit_rows,
            scratch=[terms],
        )
        slope_window = neighbours(slope_adj)
        with_gram = number == 0
        extra = [gram] if with_gram else []
        dots_shape = f32(devices, packed_rows, LANES) if with_gram else f32(devices, LANES)
        product, dots = call(
            functools.partial(slope_kernel, cap, half, groups, tiles, variables, number, with_gram),
            (f32(size, LANES), dots_shape),
            place, slope_adj, *slope_window, flux, cut, near, far, hot, state_part, current, partner, crossed,
            diag_rows, couple_rows, mixed_rows, *vectors, *extra,
            smem=(0,),
            scratch=[terms, pltpu.VMEM((LANES, LANES), jnp.float32)],
        )
        got = lax.all_to_all(dots, ("span", "dom"), 0, 0, tiled=True)
        shapes = (f32(size, LANES), f32(1, LANES))
        update = functools.partial(update_kernel, count_all, size, number, with_gram, per_row)
        if with_gram:
            current, hess, inverse = call(
                update, shapes + (f32(height, LANES),), got, product, mixed_rows,
                scratch=[pltpu.VMEM((height, LANES), jnp.float32)],
            )
        else:
            current, hess = call(update, shapes, got, product, mixed_rows, *vectors, inverse)
        hess_rows.append(hess[:, : basis + PRODUCTS])
        vectors.append(current)
        if number + 1 < PRODUCTS:
            window = neighbours(current)
        partner = send(current, swap)
        finished += [current, partner]
    stacked = call(
        functools.partial(output_kernel, half, size), f32(PRODUCTS * size, LANES), place, *finished, smem=(0,)
    )
    stacked = stacked.reshape(PRODUCTS, variables, tiles, layers, LANES)
    stacked = jnp.swapaxes(stacked, 2, 3).reshape(PRODUCTS, variables, layers, cells)
    return (stacked, jnp.concatenate(hess_rows, axis=0))


def solution(mesh):
    return jax.shard_map(
        on_device,
        mesh=mesh,
        in_specs=(
            P(None, None, "span", "dom"),
            P(None, "span", "dom"),
            P("span", "dom"),
            P(None, None, "span", "dom"),
            P("dom"),
            P("dom"),
            P("dom"),
            P("dom"),
            P(None, "dom"),
            P(None, "dom"),
            P(None, "dom"),
        ),
        out_specs=(P(None, None, "span", "dom"), P()),
        check_vma=False,
    )
```

time: 102 us -> 82 us (0.80)
  waiting for transfers between devices: 23.2 us -> 6.43 us
  starting transfers between devices: 28.1 us -> 20.1 us
  Pallas kernels: 9.04 us -> 13.9 us
  blocking collectives: 33.3 us -> 32.1 us
    ppermute x21 -> x20, waiting for transfers between devices: 23.2 us -> 6.43 us  [the longest x17 6.43 us: send(): return lax.ppermute(x, 'dom', pairs)]
    ppermute x21 -> x20, starting transfers between devices: 28.1 us -> 20.1 us  [the longest x17 18.5 us: send(): return lax.ppermute(x, 'dom', pairs)]
    pallas_call x11 -> x14, Pallas kernels: 9.04 us -> 13.9 us  [call(): pl.pallas_call(kernel, out_shape=out_shape, in_specs=specs, out_specs=out...]
    unnamed x20 -> x2, local copies, waits for them, and re-layouts: 3.99 us -> 0.01 us
    concatenate x0 -> x1, local copies, waits for them, and re-layouts: none -> 3.76 us  [on_device(): raw = jnp.concatenate(list(parts.values()), axis=0)]
    convert_element_type x0 -> x2, other arithmetic: none -> 1.46 us  [the longest x1 0.77 us: on_device(): face_cells[1].astype(jnp.float32).reshape(groups, LANES)]
    all_to_all x3, blocking collectives: 33.3 us -> 32.1 us  [on_device(): got = lax.all_to_all(dots, ('span', 'dom'), 0, 0, tiled=True)]
  transfers between devices with their start and end apart: 21 -> 20, of which waited for: 18 -> 6; matrix products, arithmetic and copies ran while one was open for 1% -> 2% of each run, Pallas kernels for 0% -> 6%
where the time goes in v2:
time: 82 us; the launch traced here: 81.6 us
  blocking collectives  32.1 us (39%)
  starting transfers between devices  20.1 us (25%)
  Pallas kernels  13.9 us (17%)
  waiting for transfers between devices  6.43 us (8%)
  local copies, waits for them, and re-layouts  5.38 us (7%)
  other arithmetic  2.13 us (3%)
    all_to_all x3, blocking collectives, on_device(): got = lax.all_to_all(dots, ('span', 'dom'), 0, 0, tiled=True)  32.1 us
    ppermute x17, starting transfers between devices, send(): return lax.ppermute(x, 'dom', pairs)  18.5 us
    pallas_call x14, Pallas kernels, call(): pl.pallas_call(kernel, out_shape=out_shape, in_specs=specs, out_specs=out...  13.9 us
    ppermute x17, waiting for transfers between devices, send(): return lax.ppermute(x, 'dom', pairs)  6.43 us
    concatenate x1, local copies, waits for them, and re-layouts, on_device(): raw = jnp.concatenate(list(parts.values()), axis=0)  3.76 us
    ppermute x3, starting transfers between devices, across(): return lax.ppermute(x, ('span', 'dom'), cross)  1.67 us
  transfers between devices with their start and end apart: 20, of which 6 were waited for; matrix products, arithmetic and copies ran while one was open for 2% of the time, Pallas kernels for 6%

profile of v2, /device:TPU:0, one launch (start us, length us, event | category | flops | bytes accessed | tf_op | source)
XLA Modules:
  0.0 81.6 jit_solution(10493653794732081027)
XLA Ops:
  0.6 0.7 convert_element_type.23
  1.3 0.7 sine_bitcast_fusion
  2.0 0.8 slice_convert_fusion
  2.8 0.7 slice.44
  3.5 3.8 %concatenate.6.raw_ref = f32[278,128]{1,0:T(8,128)S(1)} concatenate(f32[40,128]{1,0:T(8,128)S(1)} %bitcast.62, f32[40,128]{1,0:T(8,128)} %bitcast.65, f32[8,128]{1,0:T(8,128)} %bitcast.68, f32[160,128]{1,0:T(8,128)} %bitcast.63, f32[4,128]{1,0:T(4,128)S(1)} %get-tuple-element.67, f32[4,128]{1,0:T(4,128)S(1)} %get-tuple-element.66, f32[4,128]{1,0:T(4,128)} %bitcast.69, ...), dimensions={0} | concatenate | bytes 284672 | tf_op jit(solution)/shard_map/concatenate | solution.py:632
  7.3 0.5 collective-permute-start
  7.8 0.1 collective-permute-start.6
  7.8 0.1 pad_add_fusion.place_ref
  7.9 0.9 %collective-permute-done.got_ref = f32[278,128]{1,0:T(8,128)S(1)} collective-permute-done((f32[278,128]{1,0:T(8,128)S(1)}, f32[278,128]{1,0:T(8,128)S(1)}, u32[]{:S(2)}, u32[]{:S(2)}) %collective-permute-start) | collective-permute-done | bytes 142368 | tf_op jit(solution)/shard_map/ppermute | solution.py:605
  8.8 1.1 %shard_map.113 = (f32[16,2,8,128]{3,2,1,0:T(8,128)S(1)}, s32[6,512]{1,0:T(8,128)S(1)}, f32[88,128]{1,0:T(8,128)S(1)}, f32[88,128]{1,0:T(8,128)S(1)}, f32[40,128]...) custom-call(s32[2]{0:T(128)S(1)} %pad_add_fusion.place_ref, ...), custom_call_target="tpu_custom_call" | custom-call | tf_op jit(solution)/shard_map/pallas_call | solution.py:37
  9.8 2.6 %collective-permute-start.1 = (f32[88,128]{1,0:T(8,128)S(1)}, f32[88,128]{1,0:T(8,128)S(1)}, u32[]{:S(2)}, u32[]{:S(2)}) collective-permute-start(f32[88,128]{1,0:T(8,128)S(1)} %get-tuple-element.34), channel_id=1, source_target_pairs={{0,3},{1,2},{2,1},{3,0},{4,7},{5,6},{6,5},{7,4},{8,11},{9,10},{10,... | collective-permute-start | bytes 135176 | tf_op jit(solution)/shard_map/ppermute | solution.py:605
  12.5 0.4 collective-permute-start.2
  12.8 1.2 %collective-permute-start.5 = (f32[40,128]{1,0:T(8,128)S(1)}, f32[40,128]{1,0:T(8,128)S(1)}, u32[]{:S(2)}, u32[]{:S(2)}) collective-permute-start(f32[40,128]{1,0:T(8,128)S(1)} %get-tuple-element.33.x_ref.v_ref), channel_id=1, source_target_pairs={{0,17},{1,16},{2,19},{3,18},{4,21},{5,20},{6,23},{7,22},{8,25},{9,... | collective-permute-start | bytes 61448 | tf_op jit(solution)/shard_map/ppermute | solution.py:611
  14.1 0.9 %shard_map.115.hot_ref = bf16[2,256,1920]{2,1,0:T(8,128)(2,1)S(1)} custom-call(s32[6,512]{1,0:T(8,128)S(1)} %get-tuple-element.37.index_ref), custom_call_target="tpu_custom_call" | custom-call | tf_op jit(solution)/shard_map/pallas_call | solution.py:37
  15.0 0.0 collective-permute-done.1
  15.0 0.0 collective-permute-done.2
  15.0 0.1 shard_map.114
  15.2 0.8 %shard_map.116 = (f32[40,128]{1,0:T(8,128)S(1)}, f32[40,128]{1,0:T(8,128)S(1)}) custom-call(f32[40,128]{1,0:T(8,128)S(1)} %get-tuple-element.33.x_ref.v_ref, f32[40,128]{1,0:T(8,128)S(1)} %slice.45.a_ref, f32[40,128]{1,0:T(8,128)S(1)} %slice.46.b_ref, f32[16,2,8,128]{3,2,1,0:T(8,128)S(1)} %get-tuple-element.36.flux_ref, ...), custom_call_target="tpu_custom_call" | custom-call | tf_op jit(solution)/shard_map/pallas_call | solution.py:37
  16.0 0.4 collective-permute-start.4
  16.4 4.2 %collective-permute-start.3 = (f32[40,128]{1,0:T(8,128)S(1)}, f32[40,128]{1,0:T(8,128)S(1)}, u32[]{:S(2)}, u32[]{:S(2)}) collective-permute-start(f32[40,128]{1,0:T(8,128)S(1)} %get-tuple-element.42.x_ref), channel_id=1, source_target_pairs={{0,3},{1,2},{2,1},{3,0},{4,7},{5,6},{6,5},{7,4},{8,11},{9,10},{10,... | collective-permute-start | bytes 61448 | tf_op jit(solution)/shard_map/ppermute | solution.py:605
  20.6 0.6 convolution_bitcast_fusion
  21.2 0.1 reshape.76
  21.3 0.1 pad.4.rest_0_
  21.4 0.0 collective-permute-done.6.got_ref
  21.4 0.7 shard_map.117.krylov_ref
  22.1 0.0 collective-permute-done.5.cross_ref
  22.1 0.0 collective-permute-done.4.b_ref
  22.1 0.0 collective-permute-done.3.a_ref
  22.2 1.7 %shard_map.118 = (f32[40,128]{1,0:T(8,128)S(1)}, f32[32,4,128]{2,1,0:T(4,128)S(1)}) custom-call(s32[2]{0:T(128)S(1)} %pad_add_fusion.place_ref, f32[40,128]{1,0:T(8,128)S(1)} %get-tuple-element.42.x_ref, f32[40,128]{1,0:T(8,128)S(1)} %collective-permute-done.3.a_ref, f32[40,128]{1,0:T(8,128)S(1)} %collective-permute-done.4.b_ref, ...), custom_call_target="tpu_custom_call" | custom-call | tf_op jit(solution)/shard_map/pallas_call | solution.py:37
  23.8 12.4 %all_to_all.27.got_ref = f32[32,4,128]{2,1,0:T(4,128)S(1)} all-to-all(f32[32,4,128]{2,1,0:T(4,128)S(1)} %get-tuple-element.47), channel_id=1, replica_groups=mesh['span'=2,'dom'=16] {'span','dom'}, dimensions={0} | all-to-all | bytes 131072 | tf_op jit(solution)/shard_map/all_to_all | solution.py:698
  36.3 1.9 %shard_map.119 = (f32[40,128]{1,0:T(8,128)S(1)}, f32[1,128]{1,0:T(1,128)S(1)}, f32[24,128]{1,0:T(8,128)S(1)}) custom-call(f32[32,4,128]{2,1,0:T(4,128)S(1)} %all_to_all.27.got_ref, f32[40,128]{1,0:T(8,128)S(1)} %get-tuple-element.48.w_ref, f32[800,128]{1,0:T(8,128)S(1)} %shard_map.117.krylov_ref), custom_call_target="tpu_custom_call" | custom-call | tf_op jit(solution)/shard_map/pallas_call | solution.py:37
  38.2 0.2 collective-permute-start.9
  38.4 1.4 %collective-permute-start.8 = (f32[40,128]{1,0:T(8,128)S(1)}, f32[40,128]{1,0:T(8,128)S(1)}, u32[]{:S(2)}, u32[]{:S(2)}) collective-permute-start(f32[40,128]{1,0:T(8,128)S(1)} %get-tuple-element.49.x_ref.v_ref.rest_0_.refs_0_), channel_id=1, source_target_pairs={{0,3},{1,2},{2,1},{3,0},{4,7},{5,6},{6,5},{7,4},{8,11},{9,10},{10,... | collective-permute-start | bytes 61448 | tf_op jit(solution)/shard_map/ppermute | solution.py:605
  39.8 0.4 collective-permute-start.12
  40.2 0.4 collective-permute-start.7
  40.6 0.0 collective-permute-done.9.b_ref
  40.6 1.0 %collective-permute-done.8.a_ref = f32[40,128]{1,0:T(8,128)S(1)} collective-permute-done((f32[40,128]{1,0:T(8,128)S(1)}, f32[40,128]{1,0:T(8,128)S(1)}, u32[]{:S(2)}, u32[]{:S(2)}) %collective-permute-start.8) | collective-permute-done | bytes 20512 | tf_op jit(solution)/shard_map/ppermute | solution.py:605
  41.6 0.8 %shard_map.120 = (f32[40,128]{1,0:T(8,128)S(1)}, f32[40,128]{1,0:T(8,128)S(1)}) custom-call(f32[40,128]{1,0:T(8,128)S(1)} %get-tuple-element.49.x_ref.v_ref.rest_0_.refs_0_, f32[40,128]{1,0:T(8,128)S(1)} %collective-permute-done.8.a_ref, f32[40,128]{1,0:T(8,128)S(1)} %collective-permute-done.9.b_ref, f32[16,2,8,128]{3,2,1,0:T(8,128)S(1)} %get-tuple-element.36.flux_ref, ...), custom_call_target="tpu_custom_call" | custom-call | tf_op jit(solution)/shard_map/pallas_call | solution.py:37
  42.5 0.4 collective-permute-start.11
  42.9 2.4 %collective-permute-start.10 = (f32[40,128]{1,0:T(8,128)S(1)}, f32[40,128]{1,0:T(8,128)S(1)}, u32[]{:S(2)}, u32[]{:S(2)}) collective-permute-start(f32[40,128]{1,0:T(8,128)S(1)} %get-tuple-element.50.x_ref), channel_id=1, source_target_pairs={{0,3},{1,2},{2,1},{3,0},{4,7},{5,6},{6,5},{7,4},{8,11},{9,10},{10,... | collective-permute-start | bytes 61448 | tf_op jit(solution)/shard_map/ppermute | solution.py:605
  45.3 1.5 %collective-permute-done.10.a_ref = f32[40,128]{1,0:T(8,128)S(1)} collective-permute-done((f32[40,128]{1,0:T(8,128)S(1)}, f32[40,128]{1,0:T(8,128)S(1)}, u32[]{:S(2)}, u32[]{:S(2)}) %collective-permute-start.10) | collective-permute-done | bytes 20512 | tf_op jit(solution)/shard_map/ppermute | solution.py:605
  46.9 1.7 %shard_map.121 = (f32[40,128]{1,0:T(8,128)S(1)}, f32[32,128]{1,0:T(8,128)S(1)}) custom-call(s32[2]{0:T(128)S(1)} %pad_add_fusion.place_ref, f32[40,128]{1,0:T(8,128)S(1)} %get-tuple-element.50.x_ref, f32[40,128]{1,0:T(8,128)S(1)} %collective-permute-done.10.a_ref, f32[40,128]{1,0:T(8,128)S(1)} %collective-permute-done.11.b_ref, ...), custom_call_target="tpu_custom_call" | custom-call | tf_op jit(solution)/shard_map/pallas_call | solution.py:37
  48.6 9.9 %all_to_all.28 = f32[32,1,128]{2,1,0:T(1,128)S(1)} all-to-all(f32[32,1,128]{2,1,0:T(1,128)S(1)} %bitcast.58), channel_id=1, replica_groups=mesh['span'=2,'dom'=16] {'span','dom'}, dimensions={0} | all-to-all | bytes 32768 | tf_op jit(solution)/shard_map/all_to_all | solution.py:698
  58.5 0.2 shard_map.122
  58.7 0.1 collective-permute-start.15
  58.8 1.7 %collective-permute-start.14 = (f32[40,128]{1,0:T(8,128)S(1)}, f32[40,128]{1,0:T(8,128)S(1)}, u32[]{:S(2)}, u32[]{:S(2)}) collective-permute-start(f32[40,128]{1,0:T(8,128)S(1)} %get-tuple-element.55.x_ref.v_ref.rest_1_.refs_2_), channel_id=1, source_target_pairs={{0,3},{1,2},{2,1},{3,0},{4,7},{5,6},{6,5},{7,4},{8,11},{9,10},{10,... | collective-permute-start | bytes 61448 | tf_op jit(solution)/shard_map/ppermute | solution.py:605
  60.5 0.1 collective-permute-start.18
  60.5 0.6 collective-permute-start.13
  61.2 0.0 collective-permute-done.15.b_ref
  61.2 0.9 %collective-permute-done.14.a_ref = f32[40,128]{1,0:T(8,128)S(1)} collective-permute-done((f32[40,128]{1,0:T(8,128)S(1)}, f32[40,128]{1,0:T(8,128)S(1)}, u32[]{:S(2)}, u32[]{:S(2)}) %collective-permute-start.14) | collective-permute-done | bytes 20512 | tf_op jit(solution)/shard_map/ppermute | solution.py:605
  62.0 0.8 %shard_map.123 = (f32[40,128]{1,0:T(8,128)S(1)}, f32[40,128]{1,0:T(8,128)S(1)}) custom-call(f32[40,128]{1,0:T(8,128)S(1)} %get-tuple-element.55.x_ref.v_ref.rest_1_.refs_2_, f32[40,128]{1,0:T(8,128)S(1)} %collective-permute-done.14.a_ref, f32[40,128]{1,0:T(8,128)S(1)} %collective-permute-done.15.b_ref, f32[16,2,8,128]{3,2,1,0:T(8,128)S(1)} %get-tuple-element.36.flux_ref, ...), custom_call_target="tpu_custom_call" | custom-call | tf_op jit(solution)/shard_map/pallas_call | solution.py:37
  62.9 0.5 collective-permute-start.17
  63.4 2.5 %collective-permute-start.16 = (f32[40,128]{1,0:T(8,128)S(1)}, f32[40,128]{1,0:T(8,128)S(1)}, u32[]{:S(2)}, u32[]{:S(2)}) collective-permute-start(f32[40,128]{1,0:T(8,128)S(1)} %get-tuple-element.56.x_ref), channel_id=1, source_target_pairs={{0,3},{1,2},{2,1},{3,0},{4,7},{5,6},{6,5},{7,4},{8,11},{9,10},{10,... | collective-permute-start | bytes 61448 | tf_op jit(solution)/shard_map/ppermute | solution.py:605
  65.9 0.0 collective-permute-done.18.cross_ref
  65.9 0.0 collective-permute-done.13.partner_ref.refs_3_
  65.9 0.0 collective-permute-done.17.b_ref
  65.9 1.5 %collective-permute-done.16.a_ref = f32[40,128]{1,0:T(8,128)S(1)} collective-permute-done((f32[40,128]{1,0:T(8,128)S(1)}, f32[40,128]{1,0:T(8,128)S(1)}, u32[]{:S(2)}, u32[]{:S(2)}) %collective-permute-start.16) | collective-permute-done | bytes 20512 | tf_op jit(solution)/shard_map/ppermute | solution.py:605
  67.4 1.7 %shard_map.124 = (f32[40,128]{1,0:T(8,128)S(1)}, f32[32,128]{1,0:T(8,128)S(1)}) custom-call(s32[2]{0:T(128)S(1)} %pad_add_fusion.place_ref, f32[40,128]{1,0:T(8,128)S(1)} %get-tuple-element.56.x_ref, f32[40,128]{1,0:T(8,128)S(1)} %collective-permute-done.16.a_ref, f32[40,128]{1,0:T(8,128)S(1)} %collective-permute-done.17.b_ref, ...), custom_call_target="tpu_custom_call" | custom-call | tf_op jit(solution)/shard_map/pallas_call | solution.py:37
  69.1 9.8 %all_to_all.29 = f32[32,1,128]{2,1,0:T(1,128)S(1)} all-to-all(f32[32,1,128]{2,1,0:T(1,128)S(1)} %bitcast.57), channel_id=1, replica_groups=mesh['span'=2,'dom'=16] {'span','dom'}, dimensions={0} | all-to-all | bytes 32768 | tf_op jit(solution)/shard_map/all_to_all | solution.py:698
  78.9 0.2 shard_map.125
  79.1 0.1 collective-permute-start.19
  79.2 0.6 pad_maximum_fusion
  79.8 0.6 collective-permute-done.19.refs_5_
  80.4 1.2 %shard_map.126 = f32[120,128]{1,0:T(8,128)} custom-call(s32[2]{0:T(128)S(1)} %pad_add_fusion.place_ref, f32[40,128]{1,0:T(8,128)S(1)} %get-tuple-element.49.x_ref.v_ref.rest_0_.refs_0_, f32[40,128]{1,0:T(8,128)S(1)} %collective-permute-done.7.partner_ref.refs_1_, f32[40,128]{1,0:T(8,128)S(1)} %get-tuple-element.55.x_ref.v_ref.rest_1_.refs_2_, ...), custom_call_target="tpu_custom_call" | custom-call | tf_op jit(solution)/shard_map/pallas_call | solution.py:37
  (9 shorter events, 0.0 us)
Async XLA Ops:
  7.3 1.5 %collective-permute-start = (f32[278,128]{1,0:T(8,128)S(1)}, f32[278,128]{1,0:T(8,128)S(1)}, u32[]{:S(2)}, u32[]{:S(2)}) collective-permute-start(f32[278,128]{1,0:T(8,128)S(1)} %concatenate.6.raw_ref), channel_id=1, source_target_pairs={{0,1},{1,0},{2,3},{3,2},{4,5},{5,4},{6,7},{7,6},{8,9},{9,8},{10,11... | collective-permute-start | bytes 427016 | tf_op jit(solution)/shard_map/ppermute | solution.py:605
  7.8 13.6 %collective-permute-start.6 = (f32[800,128]{1,0:T(8,128)}, f32[800,128]{1,0:T(8,128)S(1)}, u32[]{:S(2)}, u32[]{:S(2)}) collective-permute-start(f32[800,128]{1,0:T(8,128)} %bitcast.53), channel_id=1, source_target_pairs={{0,1},{1,0},{2,3},{3,2},{4,5},{5,4},{6,7},{7,6},{8,9},{9,8},{10,11... | collective-permute-start | bytes 1228808 | tf_op jit(solution)/shard_map/ppermute | solution.py:605
  9.8 5.2 %collective-permute-start.1 = (f32[88,128]{1,0:T(8,128)S(1)}, f32[88,128]{1,0:T(8,128)S(1)}, u32[]{:S(2)}, u32[]{:S(2)}) collective-permute-start(f32[88,128]{1,0:T(8,128)S(1)} %get-tuple-element.34), channel_id=1, source_target_pairs={{0,3},{1,2},{2,1},{3,0},{4,7},{5,6},{6,5},{7,4},{8,11},{9,10},{10,... | collective-permute-start | bytes 135176 | tf_op jit(solution)/shard_map/ppermute | solution.py:605
  12.5 2.5 %collective-permute-start.2 = (f32[88,128]{1,0:T(8,128)S(1)}, f32[88,128]{1,0:T(8,128)S(1)}, u32[]{:S(2)}, u32[]{:S(2)}) collective-permute-start(f32[88,128]{1,0:T(8,128)S(1)} %get-tuple-element.35), channel_id=1, source_target_pairs={{0,1},{1,0},{2,5},{3,4},{4,3},{5,2},{6,9},{7,8},{8,7},{9,6},{10,13... | collective-permute-start | bytes 135176 | tf_op jit(solution)/shard_map/ppermute | solution.py:605
  12.8 9.3 %collective-permute-start.5 = (f32[40,128]{1,0:T(8,128)S(1)}, f32[40,128]{1,0:T(8,128)S(1)}, u32[]{:S(2)}, u32[]{:S(2)}) collective-permute-start(f32[40,128]{1,0:T(8,128)S(1)} %get-tuple-element.33.x_ref.v_ref), channel_id=1, source_target_pairs={{0,17},{1,16},{2,19},{3,18},{4,21},{5,20},{6,23},{7,22},{8,25},{9,... | collective-permute-start | bytes 61448 | tf_op jit(solution)/shard_map/ppermute | solution.py:611
  14.1 6.5 %copy-start = (f32[20,5,4,256]{3,2,1,0:T(4,128)S(1)}, f32[20,5,4,256]{3,2,1,0:T(4,128)}, u32[]{:S(2)}) copy-start(f32[20,5,4,256]{3,2,1,0:T(4,128)} %param.11) | copy-start | bytes 1228804
  16.0 6.1 %collective-permute-start.4 = (f32[40,128]{1,0:T(8,128)S(1)}, f32[40,128]{1,0:T(8,128)S(1)}, u32[]{:S(2)}, u32[]{:S(2)}) collective-permute-start(f32[40,128]{1,0:T(8,128)S(1)} %get-tuple-element.42.x_ref), channel_id=1, source_target_pairs={{0,1},{1,0},{2,5},{3,4},{4,3},{5,2},{6,9},{7,8},{8,7},{9,6},{10,13... | collective-permute-start | bytes 61448 | tf_op jit(solution)/shard_map/ppermute | solution.py:605
  16.4 5.7 %collective-permute-start.3 = (f32[40,128]{1,0:T(8,128)S(1)}, f32[40,128]{1,0:T(8,128)S(1)}, u32[]{:S(2)}, u32[]{:S(2)}) collective-permute-start(f32[40,128]{1,0:T(8,128)S(1)} %get-tuple-element.42.x_ref), channel_id=1, source_target_pairs={{0,3},{1,2},{2,1},{3,0},{4,7},{5,6},{6,5},{7,4},{8,11},{9,10},{10,... | collective-permute-start | bytes 61448 | tf_op jit(solution)/shard_map/ppermute | solution.py:605
  38.2 2.4 %collective-permute-start.9 = (f32[40,128]{1,0:T(8,128)S(1)}, f32[40,128]{1,0:T(8,128)S(1)}, u32[]{:S(2)}, u32[]{:S(2)}) collective-permute-start(f32[40,128]{1,0:T(8,128)S(1)} %get-tuple-element.49.x_ref.v_ref.rest_0_.refs_0_), channel_id=1, source_target_pairs={{0,1},{1,0},{2,5},{3,4},{4,3},{5,2},{6,9},{7,8},{8,7},{9,6},{10,13... | collective-permute-start | bytes 61448 | tf_op jit(solution)/shard_map/ppermute | solution.py:605
  38.4 3.2 %collective-permute-start.8 = (f32[40,128]{1,0:T(8,128)S(1)}, f32[40,128]{1,0:T(8,128)S(1)}, u32[]{:S(2)}, u32[]{:S(2)}) collective-permute-start(f32[40,128]{1,0:T(8,128)S(1)} %get-tuple-element.49.x_ref.v_ref.rest_0_.refs_0_), channel_id=1, source_target_pairs={{0,3},{1,2},{2,1},{3,0},{4,7},{5,6},{6,5},{7,4},{8,11},{9,10},{10,... | collective-permute-start | bytes 61448 | tf_op jit(solution)/shard_map/ppermute | solution.py:605
  39.8 5.5 %collective-permute-start.12 = (f32[40,128]{1,0:T(8,128)S(1)}, f32[40,128]{1,0:T(8,128)S(1)}, u32[]{:S(2)}, u32[]{:S(2)}) collective-permute-start(f32[40,128]{1,0:T(8,128)S(1)} %get-tuple-element.49.x_ref.v_ref.rest_0_.refs_0_), channel_id=1, source_target_pairs={{0,17},{1,16},{2,19},{3,18},{4,21},{5,20},{6,23},{7,22},{8,25},{9,... | collective-permute-start | bytes 61448 | tf_op jit(solution)/shard_map/ppermute | solution.py:611
  40.2 5.1 %collective-permute-start.7 = (f32[40,128]{1,0:T(8,128)S(1)}, f32[40,128]{1,0:T(8,128)S(1)}, u32[]{:S(2)}, u32[]{:S(2)}) collective-permute-start(f32[40,128]{1,0:T(8,128)S(1)} %get-tuple-element.49.x_ref.v_ref.rest_0_.refs_0_), channel_id=1, source_target_pairs={{0,1},{1,0},{2,3},{3,2},{4,5},{5,4},{6,7},{7,6},{8,9},{9,8},{10,11... | collective-permute-start | bytes 61448 | tf_op jit(solution)/shard_map/ppermute | solution.py:605
  42.5 2.9 %collective-permute-start.11 = (f32[40,128]{1,0:T(8,128)S(1)}, f32[40,128]{1,0:T(8,128)S(1)}, u32[]{:S(2)}, u32[]{:S(2)}) collective-permute-start(f32[40,128]{1,0:T(8,128)S(1)} %get-tuple-element.50.x_ref), channel_id=1, source_target_pairs={{0,1},{1,0},{2,5},{3,4},{4,3},{5,2},{6,9},{7,8},{8,7},{9,6},{10,13... | collective-permute-start | bytes 61448 | tf_op jit(solution)/shard_map/ppermute | solution.py:605
  42.9 4.0 %collective-permute-start.10 = (f32[40,128]{1,0:T(8,128)S(1)}, f32[40,128]{1,0:T(8,128)S(1)}, u32[]{:S(2)}, u32[]{:S(2)}) collective-permute-start(f32[40,128]{1,0:T(8,128)S(1)} %get-tuple-element.50.x_ref), channel_id=1, source_target_pairs={{0,3},{1,2},{2,1},{3,0},{4,7},{5,6},{6,5},{7,4},{8,11},{9,10},{10,... | collective-permute-start | bytes 61448 | tf_op jit(solution)/shard_map/ppermute | solution.py:605
  58.7 2.4 %collective-permute-start.15 = (f32[40,128]{1,0:T(8,128)S(1)}, f32[40,128]{1,0:T(8,128)S(1)}, u32[]{:S(2)}, u32[]{:S(2)}) collective-permute-start(f32[40,128]{1,0:T(8,128)S(1)} %get-tuple-element.55.x_ref.v_ref.rest_1_.refs_2_), channel_id=1, source_target_pairs={{0,1},{1,0},{2,5},{3,4},{4,3},{5,2},{6,9},{7,8},{8,7},{9,6},{10,13... | collective-permute-start | bytes 61448 | tf_op jit(solution)/shard_map/ppermute | solution.py:605
  58.8 3.3 %collective-permute-start.14 = (f32[40,128]{1,0:T(8,128)S(1)}, f32[40,128]{1,0:T(8,128)S(1)}, u32[]{:S(2)}, u32[]{:S(2)}) collective-permute-start(f32[40,128]{1,0:T(8,128)S(1)} %get-tuple-element.55.x_ref.v_ref.rest_1_.refs_2_), channel_id=1, source_target_pairs={{0,3},{1,2},{2,1},{3,0},{4,7},{5,6},{6,5},{7,4},{8,11},{9,10},{10,... | collective-permute-start | bytes 61448 | tf_op jit(solution)/shard_map/ppermute | solution.py:605
  60.5 5.4 %collective-permute-start.18 = (f32[40,128]{1,0:T(8,128)S(1)}, f32[40,128]{1,0:T(8,128)S(1)}, u32[]{:S(2)}, u32[]{:S(2)}) collective-permute-start(f32[40,128]{1,0:T(8,128)S(1)} %get-tuple-element.55.x_ref.v_ref.rest_1_.refs_2_), channel_id=1, source_target_pairs={{0,17},{1,16},{2,19},{3,18},{4,21},{5,20},{6,23},{7,22},{8,25},{9,... | collective-permute-start | bytes 61448 | tf_op jit(solution)/shard_map/ppermute | solution.py:611
  60.5 5.4 %collective-permute-start.13 = (f32[40,128]{1,0:T(8,128)S(1)}, f32[40,128]{1,0:T(8,128)S(1)}, u32[]{:S(2)}, u32[]{:S(2)}) collective-permute-start(f32[40,128]{1,0:T(8,128)S(1)} %get-tuple-element.55.x_ref.v_ref.rest_1_.refs_2_), channel_id=1, source_target_pairs={{0,1},{1,0},{2,3},{3,2},{4,5},{5,4},{6,7},{7,6},{8,9},{9,8},{10,11... | collective-permute-start | bytes 61448 | tf_op jit(solution)/shard_map/ppermute | solution.py:605
  62.9 3.0 %collective-permute-start.17 = (f32[40,128]{1,0:T(8,128)S(1)}, f32[40,128]{1,0:T(8,128)S(1)}, u32[]{:S(2)}, u32[]{:S(2)}) collective-permute-start(f32[40,128]{1,0:T(8,128)S(1)} %get-tuple-element.56.x_ref), channel_id=1, source_target_pairs={{0,1},{1,0},{2,5},{3,4},{4,3},{5,2},{6,9},{7,8},{8,7},{9,6},{10,13... | collective-permute-start | bytes 61448 | tf_op jit(solution)/shard_map/ppermute | solution.py:605
  63.4 4.0 %collective-permute-start.16 = (f32[40,128]{1,0:T(8,128)S(1)}, f32[40,128]{1,0:T(8,128)S(1)}, u32[]{:S(2)}, u32[]{:S(2)}) collective-permute-start(f32[40,128]{1,0:T(8,128)S(1)} %get-tuple-element.56.x_ref), channel_id=1, source_target_pairs={{0,3},{1,2},{2,1},{3,0},{4,7},{5,6},{6,5},{7,4},{8,11},{9,10},{10,... | collective-permute-start | bytes 61448 | tf_op jit(solution)/shard_map/ppermute | solution.py:605
  79.1 1.3 %collective-permute-start.19 = (f32[40,128]{1,0:T(8,128)S(1)}, f32[40,128]{1,0:T(8,128)S(1)}, u32[]{:S(2)}, u32[]{:S(2)}) collective-permute-start(f32[40,128]{1,0:T(8,128)S(1)} %get-tuple-element.60.refs_4_), channel_id=1, source_target_pairs={{0,1},{1,0},{2,3},{3,2},{4,5},{5,4},{6,7},{7,6},{8,9},{9,8},{10,11... | collective-permute-start | bytes 61448 | tf_op jit(solution)/shard_map/ppermute | solution.py:605
